TPU v7x, 256 devices: a whole 4x4x8 slice. The times are simulated.
256 devices in a mesh: kv: 8 (over x, core), seq: 8 (over z), vocab: 4 (over y).
Axes of the slice: x: 4, y: 4, z: 8, core: 2. Of those that a mesh axis runs over, the one named last changes fastest.
Arguments:
- hidden_state: bfloat16 [48, 4, 3584], P('kv', 'vocab', 'seq'), may hold values from -6 to 6
- input_projection: bfloat16 [3584, 8, 1024], P('seq', 'kv'), may hold values from -0.09375 to 0.09375
- output_projection: bfloat16 [8, 512, 3584], P('kv', None, 'seq'), may hold values from -0.09375 to 0.09375
- norm_pre_attention: float32 [3584], P('seq'), may hold values from 0.1 to 1.9
- norm_post_attention: float32 [3584], P('seq'), may hold values from 0.1 to 1.9
- norm_pre_feedforward: float32 [3584], P('seq'), may hold values from 0.1 to 1.9
- norm_post_feedforward: float32 [3584], P('seq'), may hold values from 0.1 to 1.9
- norm_final: float32 [3584], P('seq'), may hold values from 0.1 to 1.9
- cache_keys: bfloat16 [4, 16384, 8, 256], P('vocab', 'seq', 'kv')
- cache_values: bfloat16 [4, 16384, 8, 256], P('vocab', 'seq', 'kv')
- cache_length: int32 [4], P('vocab'), may hold values from 1 to 16379, as said below
- ancestors: int32 [4, 48, 48], P('vocab'), may hold values from 0 to 1, as said below
- accepted_path: int32 [4, 5], P('vocab'), may hold values from 0 to 47, as said below
- gate_up_weight: bfloat16 [3584, 2, 14336], P('seq', None, ('kv', 'vocab')), may hold values from -0.09375 to 0.09375
- down_weight: bfloat16 [14336, 3584], P(('kv', 'vocab'), 'seq'), may hold values from -0.046875 to 0.046875
- draft_weight: bfloat16 [4, 3584, 3584], P(None, 'seq', ('kv', 'vocab')), may hold values from -0.09375 to 0.09375
- draft_bias: float32 [4, 3584], P(None, ('kv', 'vocab')), may hold values from -3 to 3
- vocab_weight: bfloat16 [131072, 3584], P(('kv', 'seq', 'vocab'))
- candidate_tokens: int32 [5, 48, 4, 8], replicated, may hold values from 0 to 131071
Outputs:
- keys_updated: bfloat16 [4, 16384, 8, 256], P('vocab', 'seq', 'kv')
- values_updated: bfloat16 [4, 16384, 8, 256], P('vocab', 'seq', 'kv')
- log_normalizer: float32 [5, 48, 4], replicated
- candidate_logits: float32 [5, 48, 4, 8], replicated
Inputs may be any that keep to these rules, and one draw needn't show every extreme that they name: The first cache_length[k] slots of tenant k's cache are filled; in every draw some tenant holds exactly 16379. ancestors[k, t, u] is 1 exactly when u is t or an ancestor of t in tenant k's tree; node 0 is the root and every parent has a lower index than its child. accepted_path[k] lists 5 nodes of tenant k's tree from the root down, each the parent of the next; the last of them is node 47.
All inputs are finite; a program needn't handle non-finite values.
Results may differ from a plain program's by a relative error of at most 0.02.
Values may be sent and summed in bfloat16 or wider, within the bound.
A program may use at most 64 MiB of HBM per device.

v0:
```python
import jax
import jax.numpy as jnp
from jax import lax
from jax.sharding import PartitionSpec as P

MODEL_WIDTH = 3584
HEAD_SIZE = 256
CAND = 8


EPSILON = 1e-06
SCORE_CAP = 50.0
LOGIT_CAP = 30.0


def apply_rotary(vectors, token_positions):
    half_dim = vectors.shape[-1] // 2
    frequency = 10000.0 ** (-2.0 * jnp.arange(half_dim, dtype=jnp.float32) / vectors.shape[-1])
    angles = token_positions.astype(jnp.float32)[..., None] * frequency
    cosine = jnp.cos(angles)
    sine_part = jnp.sin(angles)
    first_half = vectors[..., :half_dim]
    second_half = vectors[..., half_dim:]
    return jnp.concatenate(
        [
            first_half * cosine - second_half * sine_part,
            second_half * cosine + first_half * sine_part,
        ],
        axis=-1,
    )


def capped_weight(scores):
    return jnp.exp(SCORE_CAP * jnp.tanh(scores * 0.0625 / SCORE_CAP))


def row_inverse(values):
    totals = lax.psum(jnp.sum(values * values, axis=-1), "seq")
    return lax.rsqrt(totals / MODEL_WIDTH + EPSILON)[:, None]


def gated_units(gate_up, squares):
    inverse = lax.rsqrt(squares / MODEL_WIDTH + EPSILON)[:, None]
    return (
        jax.nn.gelu(gate_up[:, 0] * inverse, approximate=True) * (gate_up[:, 1] * inverse)
    ).astype(jnp.bfloat16)


def local(
    hidden_state,
    input_projection,
    output_projection,
    norm_pre_attention,
    norm_post_attention,
    norm_pre_feedforward,
    norm_post_feedforward,
    norm_final,
    cache_keys,
    cache_values,
    cache_length,
    ancestors,
    accepted_path,
    gate_up_weight,
    down_weight,
    draft_weight,
    draft_bias,
    vocab_weight,
    candidate_tokens,
):
    tok_block = hidden_state.shape[0]
    kv_count = lax.axis_size("kv")
    tenants = lax.axis_size("vocab")
    tree_size = tok_block * kv_count
    own_state = hidden_state[:, 0, :]
    tenant_state = lax.all_gather(own_state, "kv", axis=0, tiled=True)
    tenant_float = tenant_state.astype(jnp.float32)
    scaled_input = (tenant_float * norm_pre_attention).astype(jnp.bfloat16)
    projected_rows = jnp.einsum(
        "td,dhc->thc", scaled_input, input_projection, preferred_element_type=jnp.float32
    )
    projected_rows, squares = lax.psum(
        (projected_rows, jnp.sum(tenant_float * tenant_float, axis=-1)), "seq"
    )
    projected_rows = projected_rows * lax.rsqrt(squares / MODEL_WIDTH + EPSILON)[:, None, None]
    head_count = projected_rows.shape[1]
    depths = jnp.sum(ancestors[0], axis=-1) - 1
    length = cache_length[0]
    token_positions = length + depths
    query_rows = apply_rotary(
        projected_rows[:, :, : 2 * HEAD_SIZE].reshape(tree_size, head_count, 2, HEAD_SIZE),
        token_positions[:, None, None],
    ).astype(jnp.bfloat16)
    new_keys = apply_rotary(
        projected_rows[:, :, 2 * HEAD_SIZE : 3 * HEAD_SIZE], token_positions[:, None]
    ).astype(jnp.bfloat16)
    new_values = projected_rows[:, :, 3 * HEAD_SIZE :].astype(jnp.bfloat16)
    block_size = cache_keys.shape[1]
    block_start = lax.axis_index("seq") * block_size
    cache_cells = block_start + jnp.arange(block_size, dtype=jnp.int32)
    scores = jnp.einsum(
        "thgc,shc->thgs", query_rows, cache_keys[0], preferred_element_type=jnp.float32
    )
    weights = jnp.where((cache_cells < length)[None, None, None, :], capped_weight(scores), 0.0)
    numerator = jnp.einsum(
        "thgs,shc->thgc",
        weights.astype(jnp.bfloat16),
        cache_values[0],
        preferred_element_type=jnp.float32,
    )
    numerator, denominator = lax.psum((numerator, jnp.sum(weights, axis=-1)), "seq")
    tree_scores = jnp.einsum(
        "thgc,uhc->thgu", query_rows, new_keys, preferred_element_type=jnp.float32
    )
    tree_weights = jnp.where(ancestors[0][:, None, None, :] > 0, capped_weight(tree_scores), 0.0)
    numerator = numerator + jnp.einsum(
        "thgu,uhc->thgc",
        tree_weights.astype(jnp.bfloat16),
        new_values,
        preferred_element_type=jnp.float32,
    )
    denominator = denominator + jnp.sum(tree_weights, axis=-1)
    attended = (
        (numerator / denominator[..., None])
        .astype(jnp.bfloat16)
        .reshape(tree_size, head_count * 2 * HEAD_SIZE)
    )
    out_matrix = output_projection.reshape(head_count * 2 * HEAD_SIZE, output_projection.shape[2])
    attention_out = lax.psum_scatter(
        jnp.dot(attended, out_matrix, preferred_element_type=jnp.float32),
        "kv",
        scatter_dimension=0,
        tiled=True,
    )
    first_sum = (
        own_state.astype(jnp.float32)
        + attention_out * row_inverse(attention_out) * norm_post_attention
    ).astype(jnp.bfloat16)
    all_state = lax.all_gather(first_sum, ("kv", "vocab"), axis=0, tiled=True)
    all_float = all_state.astype(jnp.float32)
    scaled_ffn = (all_float * norm_pre_feedforward).astype(jnp.bfloat16)
    gate_up = jnp.einsum(
        "td,dcf->tcf", scaled_ffn, gate_up_weight, preferred_element_type=jnp.float32
    )
    ffn_squares = jnp.sum(all_float * all_float, axis=-1)
    gate_up, ffn_squares = lax.psum((gate_up, ffn_squares), "seq")
    activated = gated_units(gate_up, ffn_squares)
    ffn_out = lax.psum_scatter(
        jnp.dot(activated, down_weight, preferred_element_type=jnp.float32),
        ("kv", "vocab"),
        scatter_dimension=0,
        tiled=True,
    )
    first_float = first_sum.astype(jnp.float32)
    second_sum = (first_float + ffn_out * row_inverse(ffn_out) * norm_post_feedforward).astype(
        jnp.bfloat16
    )
    second_float = second_sum.astype(jnp.float32)
    normed = (second_float * row_inverse(second_float) * norm_final).astype(jnp.bfloat16)
    gathered = lax.all_gather(normed, ("kv", "vocab"), axis=0, tiled=True)
    lifted = jnp.einsum("td,ndc->tnc", gathered, draft_weight, preferred_element_type=jnp.float32)
    lifted = lax.psum(lifted.astype(jnp.bfloat16), "seq").astype(jnp.float32)
    branch = jax.nn.silu(lifted + draft_bias).astype(jnp.bfloat16)
    row_count = gathered.shape[0]
    vocab_rows = vocab_weight.shape[0]
    draft_count = branch.shape[1]
    columns = vocab_weight
    base_logits = lax.dot_general(
        lax.all_gather(gathered, "seq", axis=1, tiled=True),
        columns,
        (((1,), (1,)), ((), ())),
        preferred_element_type=jnp.float32,
    )
    columns = vocab_weight
    draft_extra = jnp.einsum(
        "tnc,vc->tnv",
        lax.all_gather(branch, ("kv", "vocab"), axis=2, tiled=True),
        columns,
        preferred_element_type=jnp.float32,
    )
    raw_logits = jnp.concatenate(
        [base_logits[:, None, :], base_logits[:, None, :] + draft_extra], axis=1
    )
    logits = LOGIT_CAP * jnp.tanh(raw_logits / LOGIT_CAP)
    totals = jnp.sum(jnp.exp(logits), axis=-1)
    head_total = draft_count + 1
    candidates = candidate_tokens.reshape(head_total, kv_count, tok_block, tenants, CAND)
    candidates = jnp.transpose(candidates, (0, 1, 3, 2, 4)).reshape(head_total, row_count, CAND)
    candidates = jnp.transpose(candidates, (1, 0, 2))
    vocab_start = lax.axis_index(("kv", "seq", "vocab")) * vocab_rows
    local_tokens = candidates - vocab_start
    entry_index = jnp.arange(vocab_rows, dtype=jnp.int32)
    picked = jnp.stack(
        [
            jnp.sum(
                jnp.where(entry_index == local_tokens[:, :, column : column + 1], logits, 0.0),
                axis=-1,
            )
            for column in range(CAND)
        ],
        axis=-1,
    )
    totals, picked = lax.psum((totals, picked), ("kv", "seq", "vocab"))
    log_totals = jnp.transpose(jnp.log(totals)).reshape(head_total, kv_count, tenants, tok_block)
    log_normalizer = jnp.transpose(log_totals, (0, 1, 3, 2)).reshape(head_total, tree_size, tenants)
    picked = jnp.transpose(picked, (1, 0, 2)).reshape(
        head_total, kv_count, tenants, tok_block, CAND
    )
    candidate_logits = jnp.transpose(picked, (0, 1, 3, 2, 4)).reshape(
        head_total, tree_size, tenants, CAND
    )
    accept_count = accepted_path.shape[1]
    slot_rows = length + jnp.arange(accept_count, dtype=jnp.int32)
    tree_nodes = jnp.arange(tree_size, dtype=jnp.int32)
    matches = (cache_cells[:, None, None] == slot_rows[None, :, None]) & (
        accepted_path[0][None, :, None] == tree_nodes[None, None, :]
    )
    selector = jnp.sum(matches.astype(jnp.float32), axis=1)
    written = jnp.sum(selector, axis=-1) > 0.0
    selector = selector.astype(jnp.bfloat16)

    def write_path(old_block, fresh_rows):
        moved_rows = jnp.dot(
            selector, fresh_rows.reshape(tree_size, -1), preferred_element_type=jnp.float32
        ).astype(jnp.bfloat16)
        return jnp.where(
            written[:, None], moved_rows, old_block[0].reshape(block_size, -1)
        ).reshape(old_block.shape)

    keys_updated = write_path(cache_keys, new_keys)
    values_updated = write_path(cache_values, new_values)
    return (keys_updated, values_updated, log_normalizer, candidate_logits)


def solution(mesh):
    placed = (
        P("kv", "vocab", "seq"),
        P("seq", "kv", None),
        P("kv", None, "seq"),
        P("seq"),
        P("seq"),
        P("seq"),
        P("seq"),
        P("seq"),
        P("vocab", "seq", "kv", None),
        P("vocab", "seq", "kv", None),
        P("vocab"),
        P("vocab", None, None),
        P("vocab", None),
        P("seq", None, ("kv", "vocab")),
        P(("kv", "vocab"), "seq"),
        P(None, "seq", ("kv", "vocab")),
        P(None, ("kv", "vocab")),
        P(("kv", "seq", "vocab"), None),
        P(),
    )
    return jax.shard_map(
        local,
        mesh=mesh,
        in_specs=placed,
        out_specs=(P("vocab", "seq", "kv", None), P("vocab", "seq", "kv", None), P(), P()),
        check_vma=False,
    )
```

profile of v0, /device:TPU:1, one launch (start us, length us, event | category | flops | bytes accessed | tf_op | source)
XLA Modules:
  0.0 775.7 jit_solution(17245792410160348582)
XLA Ops:
  8.1 15.8 %all-gather = bf16[48,1,448]{2,1,0:T(2,128)(2,1)S(1)} all-gather(bf16[6,1,448]{2,1,0:T(2,128)(2,1)S(1)} %copy.52), channel_id=2, replica_groups=mesh['kv'=8,'seq'=8,'vocab'=4] {'kv'}, dimensions={0}, use_global_device_ids=true | all-gather | bytes 48384 | tf_op jit(solution)/shard_map/all_gather | solution.py:75
  24.0 2.2 convolution_bitcast_fusion
  26.3 15.0 %psum.85 = f32[48]{0:T(128)S(1)} all-reduce(f32[48]{0:T(128)S(1)} %fusion.56), channel_id=1, replica_groups=mesh['kv'=8,'seq'=8,'vocab'=4] {'seq'}, use_global_device_ids=true, to_apply=%region_4.5 | all-reduce | flops 48 | bytes 384 | tf_op jit(solution)/shard_map/psum | solution.py:81
  43.9 50.6 %all-reduce.10.cloned.1.call-done = f32[48,1,1024]{2,0,1:T(8,128)} async-done(((f32[48,1,1024]{2,0,1:T(8,128)}), f32[48,1,1024]{2,0,1:T(8,128)}) %all-reduce.10.cloned.1.call-update) | async-done | bytes 196624 | tf_op jit(solution)/shard_map/psum | solution.py:81
  97.1 12.7 %psum.87 = f32[48,1,2]{0,2,1:T(2,128)S(1)} all-reduce(f32[48,1,2]{0,2,1:T(2,128)S(1)} %bitcast.224), channel_id=1, replica_groups=mesh['kv'=8,'seq'=8,'vocab'=4] {'seq'}, use_global_device_ids=true, to_apply=%region_8.9 | all-reduce | flops 96 | bytes 768 | tf_op jit(solution)/shard_map/psum | solution.py:110
  109.8 2.0 convolution_bitcast_fusion.1
  112.0 73.8 %all-reduce.12.cloned.1.call-done = f32[48,1,2,256]{3,0,2,1:T(8,128)} async-done(((f32[48,1,2,256]{3,0,2,1:T(8,128)}), f32[48,1,2,256]{3,0,2,1:T(8,128)}) %all-reduce.12.cloned.1.call-update) | async-done | bytes 98320 | tf_op jit(solution)/shard_map/psum | solution.py:110
  187.3 18.1 %fusion = f32[8,448]{1,0:T(8,128)S(1)} fusion(f32[48,448]{1,0:T(8,128)S(1)} %fusion.35), kind=kCustom, calls=%all-reduce-scatter | all-reduce-scatter fusion | flops 28673 | bytes 101376
  205.3 3.4 collective-permute-start
  212.0 11.6 %psum.88 = f32[6]{0:T(128)S(1)} all-reduce(f32[6]{0:T(128)S(1)} %multiply_reduce_fusion.2), channel_id=1, replica_groups=mesh['kv'=8,'seq'=8,'vocab'=4] {'seq'}, use_global_device_ids=true, to_apply=%region_12.13 | all-reduce | flops 6 | bytes 48 | tf_op jit(solution)/shard_map/psum | solution.py:38
  223.7 45.5 %all-gather.1 = bf16[32,6,448]{2,1,0:T(8,128)(2,1)S(1)} all-gather(bf16[1,6,448]{2,1,0:T(8,128)(2,1)S(1)} %bitcast.223), channel_id=1, replica_groups=mesh['kv'=8,'seq'=8,'vocab'=4] {'kv','vocab'}, dimensions={0}, use_global_device_ids=true | all-gather | bytes 177408 | tf_op jit(solution)/shard_map/all_gather | solution.py:138
  270.8 11.5 %psum.90 = f32[192]{0:T(256)S(1)} all-reduce(f32[192]{0:T(256)S(1)} %multiply_reduce_fusion), channel_id=1, replica_groups=mesh['kv'=8,'seq'=8,'vocab'=4] {'seq'}, use_global_device_ids=true, to_apply=%region_15.16 | all-reduce | flops 192 | bytes 1536 | tf_op jit(solution)/shard_map/psum | solution.py:145
  282.3 57.1 %all-reduce.14.cloned.1.call-done = f32[192,2,448]{2,0,1:T(8,128)} async-done(((f32[192,2,448]{2,0,1:T(8,128)}), f32[192,2,448]{2,0,1:T(8,128)}) %all-reduce.14.cloned.1.call-update) | async-done | bytes 688144 | tf_op jit(solution)/shard_map/psum | solution.py:145
  341.1 68.1 %fusion.1 = f32[8,448]{1,0:T(8,128)S(1)} fusion(f32[192,448]{1,0:T(8,128)S(1)} %fusion.53), kind=kCustom, calls=%all-reduce-scatter.1 | all-reduce-scatter fusion | flops 114689 | bytes 359424
  411.1 1.9 collective-permute-start.3
  414.4 1.9 collective-permute-start.4
  418.3 5.9 collective-permute-start.6
  424.2 6.8 collective-permute-start.7
  431.0 3.9 collective-permute-start.8
  437.2 12.6 %psum.91 = f32[6]{0:T(128)S(1)} all-reduce(f32[6]{0:T(128)S(1)} %multiply_reduce_fusion.1), channel_id=1, replica_groups=mesh['kv'=8,'seq'=8,'vocab'=4] {'seq'}, use_global_device_ids=true, to_apply=%region_18.19 | all-reduce | flops 6 | bytes 48 | tf_op jit(solution)/shard_map/psum | solution.py:38
  450.0 10.7 %psum.92 = f32[6]{0:T(128)S(1)} all-reduce(f32[6]{0:T(128)S(1)} %get-tuple-element.17), channel_id=1, replica_groups=mesh['kv'=8,'seq'=8,'vocab'=4] {'seq'}, use_global_device_ids=true, to_apply=%region_20.21 | all-reduce | flops 6 | bytes 48 | tf_op jit(solution)/shard_map/psum | solution.py:38
  460.8 48.2 %all-gather.2 = bf16[32,6,448]{2,1,0:T(8,128)(2,1)S(1)} all-gather(bf16[1,6,448]{2,1,0:T(8,128)(2,1)S(1)} %fusion.82), channel_id=1, replica_groups=mesh['kv'=8,'seq'=8,'vocab'=4] {'kv','vocab'}, dimensions={0}, use_global_device_ids=true | all-gather | bytes 177408 | tf_op jit(solution)/shard_map/all_gather | solution.py:159
  511.2 64.1 %all-reduce.16.cloned.1.call-done = bf16[192,4,112]{2,0,1:T(8,128)(2,1)} async-done(((bf16[192,4,112]{2,0,1:T(8,128)(2,1)}), bf16[192,4,112]{2,0,1:T(8,128)(2,1)}) %all-reduce.16.cloned.1.call-update) | async-done | bytes 172048 | tf_op jit(solution)/shard_map/psum | solution.py:161
  581.5 2.5 fusion.6
  585.5 30.5 %all-gather.9.cloned.1.call-done = bf16[8,448,192]{1,2,0:T(8,128)(2,1)} async-done(((bf16[1,448,192]{1,2,0:T(8,128)(2,1)}), bf16[8,448,192]{1,2,0:T(8,128)(2,1)}) %all-gather.9.cloned.1.call-update) | async-done | bytes 1376272 | tf_op jit(solution)/shard_map/all_gather | solution.py:168
  616.1 2.3 copy.59
  618.4 2.7 reshape.412
  621.1 3.8 fusion.95
  625.0 52.4 %all-gather.7.cloned.1.call-done = bf16[192,4,3584]{0,1,2:T(4,128)(2,1)} async-done(((bf16[192,4,112]{0,1,2:T(4,128)(2,1)}), bf16[192,4,3584]{0,1,2:T(4,128)(2,1)}) %all-gather.7.cloned.1.call-update) | async-done | bytes 5505040 | tf_op jit(solution)/shard_map/all_gather | solution.py:176
  677.3 8.2 %fusion.17 = f32[192,4,512]{2,0,1:T(8,128)S(1)} fusion(bf16[512,3584]{1,0:T(8,128)(2,1)} %param.36, bf16[192,4,3584]{0,1,2:T(4,128)(2,1)} %all-gather.7.cloned.1.call-done, f32[192,512]{1,0:T(8,128)S(1)} %fusion.95), kind=kOutput, calls=%fused_computation.38 | convolution fusion | flops 2818965504 | bytes 11141120 | tf_op jit(solution)/shard_map/tnc,vc->tnv/dot_general | solution.py:174
  685.6 4.4 select_reduce_fusion
  691.4 76.6 %all-reduce.4 = (f32[192,5]{0,1:T(8,128)S(1)}, f32[5,48,4,8]{1,3,2,0:T(8,128)}) all-reduce(f32[192,5]{0,1:T(8,128)S(1)} %get-tuple-element.19, f32[5,48,4,8]{1,3,2,0:T(8,128)S(1)} %reshape.401), channel_id=1, replica_groups=mesh['kv'=8,'seq'=8,'vocab'=4] {'kv','seq','vocab'}, use_global_device_ids=true, to_apply=%region_23.24 | all-reduce | flops 8640 | bytes 69120 | tf_op jit(solution)/shard_map/psum | solution.py:202
  (150 shorter events, 32.0 us)
Async XLA Ops:
  7.2 262.2 %copy-start = (bf16[448,2,448]{2,1,0:T(2,128)(2,1)S(1)}, bf16[448,2,448]{2,1,0:T(2,128)(2,1)}, u32[]{:S(2)}) copy-start(bf16[448,2,448]{2,1,0:T(2,128)(2,1)} %param.32) | copy-start | bytes 2408452
  7.2 88.7 %copy-start.2 = (bf16[1,2048,1,256]{3,1,2,0:T(8,128)(2,1)S(1)}, bf16[1,2048,1,256]{3,1,2,0:T(8,128)(2,1)}, u32[]{:S(2)}) copy-start(bf16[1,2048,1,256]{3,1,2,0:T(8,128)(2,1)} %param.27) | copy-start | bytes 3145732
  7.2 87.3 %all-reduce.10.cloned.1.call-start = ((), (), s32[]{:S(2)}) async-start(), calls=%async_computation | async-start | bytes 393216 | tf_op jit(solution)/shard_map/psum | solution.py:81
  26.1 83.6 %copy-start.1 = (bf16[1,2048,1,256]{3,1,2,0:T(8,128)(2,1)S(1)}, bf16[1,2048,1,256]{3,1,2,0:T(8,128)(2,1)}, u32[]{:S(2)}) copy-start(bf16[1,2048,1,256]{3,1,2,0:T(8,128)(2,1)} %param.28) | copy-start | bytes 3145732
  26.2 159.7 %all-reduce.12.cloned.1.call-start = ((), (), s32[]{:S(2)}) async-start(), calls=%async_computation.1 | async-start | bytes 196608 | tf_op jit(solution)/shard_map/psum | solution.py:110
  97.1 89.9 %copy-start.3 = (bf16[1,512,448]{1,2,0:T(8,128)(2,1)S(1)}, bf16[1,512,448]{1,2,0:T(8,128)(2,1)}, u32[]{:S(2)}) copy-start(bf16[1,512,448]{1,2,0:T(8,128)(2,1)} %param.21) | copy-start | bytes 1376260
  97.1 113.3 %copy-start.20 = (u32[256]{0:T(256)S(1)}, u32[256]{0:T(256)}, u32[]{:S(2)}) copy-start(u32[256]{0:T(256)} %constant.87) | copy-start | bytes 3076
  97.1 126.5 %copy-start.13 = (bf16[6,1,448]{2,0,1:T(8,128)(2,1)S(1)}, bf16[6,1,448]{2,0,1:T(8,128)(2,1)}, u32[]{:S(2)}) copy-start(bf16[6,1,448]{2,0,1:T(8,128)(2,1)} %param.19) | copy-start | bytes 16132
  97.1 126.5 %copy-start.16 = (f32[448]{0:T(512)S(1)}, f32[448]{0:T(512)}, u32[]{:S(2)}) copy-start(f32[448]{0:T(512)} %param.23) | copy-start | bytes 5380
  109.8 159.6 %copy-start.14 = (f32[448]{0:T(512)S(1)}, f32[448]{0:T(512)}, u32[]{:S(2)}) copy-start(f32[448]{0:T(512)} %param.24) | copy-start | bytes 5380
  111.8 227.7 %all-reduce.14.cloned.1.call-start = ((), (), s32[]{:S(2)}) async-start(), calls=%async_computation.2 | async-start | bytes 1572864 | tf_op jit(solution)/shard_map/psum | solution.py:145
  205.3 6.3 collective-permute-start
  208.8 2.8 collective-permute-start.1
  270.6 164.4 %copy-start.19 = (u32[256]{0:T(256)S(1)}, u32[256]{0:T(256)}, u32[]{:S(2)}) copy-start(u32[256]{0:T(256)} %constant.91) | copy-start | bytes 3076
  270.6 179.2 %copy-start.17 = (f32[448]{0:T(512)S(1)}, f32[448]{0:T(512)}, u32[]{:S(2)}) copy-start(f32[448]{0:T(512)} %param.25) | copy-start | bytes 5380
  270.6 190.1 %copy-start.18 = (f32[448]{0:T(512)S(1)}, f32[448]{0:T(512)}, u32[]{:S(2)}) copy-start(f32[448]{0:T(512)} %param.26) | copy-start | bytes 5380
  270.6 238.5 %copy-start.4 = (bf16[4,448,112]{2,1,0:T(8,128)(2,1)S(1)}, bf16[4,448,112]{2,1,0:T(8,128)(2,1)}, u32[]{:S(2)}) copy-start(bf16[4,448,112]{2,1,0:T(8,128)(2,1)} %param.34) | copy-start | bytes 1204228
  270.7 304.6 %all-reduce.16.cloned.1.call-start = ((), (), s32[]{:S(2)}) async-start(), calls=%async_computation.3 | async-start | bytes 393216 | tf_op jit(solution)/shard_map/psum | solution.py:161
  341.1 234.2 %copy-start.15 = (f32[4,112]{1,0:T(4,128)S(1)}, f32[4,112]{1,0:T(4,128)}, u32[]{:S(2)}) copy-start(f32[4,112]{1,0:T(4,128)} %param.35) | copy-start | bytes 5380
  409.1 15.1 %collective-permute-start.2 = (f32[8,448]{1,0:T(8,128)S(1)}, f32[8,448]{1,0:T(8,128)S(1)}, u32[]{:S(2)}, u32[]{:S(2)}) collective-permute-start(f32[8,448]{1,0:T(8,128)S(1)} %fusion.1), channel_id=1, source_target_pairs={{0,1},{1,2},{2,3},{3,32},{32,33},{33,34},{34,35},{35,64},{64,65},{... | collective-permute-start | bytes 43016
  411.1 20.0 %collective-permute-start.3 = (f32[8,448]{1,0:T(8,128)S(1)}, f32[8,448]{1,0:T(8,128)S(1)}, u32[]{:S(2)}, u32[]{:S(2)}) collective-permute-start(f32[8,448]{1,0:T(8,128)S(1)} %fusion.1), channel_id=1, source_target_pairs={{0,2},{1,3},{2,32},{3,33},{32,34},{33,35},{34,64},{35,65},{64,66},... | collective-permute-start | bytes 43016
  413.0 164.3 %copy-start.5 = (s32[5,48,4,8]{1,3,2,0:T(8,128)S(1)}, s32[5,48,4,8]{1,3,2,0:T(8,128)}, u32[]{:S(2)}) copy-start(s32[5,48,4,8]{1,3,2,0:T(8,128)} %param.37) | copy-start | bytes 92164
  413.0 5.3 collective-permute-start.9
  414.4 21.8 %collective-permute-start.4 = (f32[8,448]{1,0:T(8,128)S(1)}, f32[8,448]{1,0:T(8,128)S(1)}, u32[]{:S(2)}, u32[]{:S(2)}) collective-permute-start(f32[8,448]{1,0:T(8,128)S(1)} %fusion.1), channel_id=1, source_target_pairs={{0,3},{1,32},{2,33},{3,34},{32,35},{33,64},{34,65},{35,66},{64,67}... | collective-permute-start | bytes 43016
  416.4 19.9 %collective-permute-start.5 = (f32[8,448]{1,0:T(8,128)S(1)}, f32[8,448]{1,0:T(8,128)S(1)}, u32[]{:S(2)}, u32[]{:S(2)}) collective-permute-start(f32[8,448]{1,0:T(8,128)S(1)} %fusion.1), channel_id=1, source_target_pairs={{0,32},{1,33},{2,34},{3,35},{32,64},{33,65},{34,66},{35,67},{64,96... | collective-permute-start | bytes 43016
  418.3 17.9 %collective-permute-start.6 = (f32[8,448]{1,0:T(8,128)S(1)}, f32[8,448]{1,0:T(8,128)S(1)}, u32[]{:S(2)}, u32[]{:S(2)}) collective-permute-start(f32[8,448]{1,0:T(8,128)S(1)} %fusion.1), channel_id=1, source_target_pairs={{0,33},{1,34},{2,35},{3,64},{32,65},{33,66},{34,67},{35,96},{64,97... | collective-permute-start | bytes 43016
  424.2 12.1 %collective-permute-start.7 = (f32[8,448]{1,0:T(8,128)S(1)}, f32[8,448]{1,0:T(8,128)S(1)}, u32[]{:S(2)}, u32[]{:S(2)}) collective-permute-start(f32[8,448]{1,0:T(8,128)S(1)} %fusion.1), channel_id=1, source_target_pairs={{0,34},{1,35},{2,64},{3,65},{32,66},{33,67},{34,96},{35,97},{64,98... | collective-permute-start | bytes 43016
  431.0 5.2 collective-permute-start.8
  510.1 106.0 %all-gather.9.cloned.1.call-start = ((), (), s32[]{:S(2)}) async-start(), calls=%async_computation.5 | async-start | bytes 1769472 | tf_op jit(solution)/shard_map/all_gather | solution.py:168
  511.0 67.6 %copy-start.21 = (s32[1,5]{1,0:T(1,128)S(1)}, s32[1,5]{1,0:T(1,128)}, u32[]{:S(2)}) copy-start(s32[1,5]{1,0:T(1,128)} %param.31) | copy-start | bytes 64
  511.0 166.3 %all-gather.7.cloned.1.call-start = ((), (), s32[]{:S(2)}) async-start(), calls=%async_computation.4 | async-start | bytes 7569408 | tf_op jit(solution)/shard_map/all_gather | solution.py:176
  624.9 60.7 %copy-start.6 = (s32[192,5]{0,1:T(8,128)S(1)}, s32[192,5]{0,1:T(8,128)}, u32[]{:S(2)}) copy-start(s32[192,5]{0,1:T(8,128)} %get-tuple-element.43) | copy-start | bytes 11524
  (6 other events, 364.0 us)
Sparse Core Ops, SparseCore 0:
  26.3 68.1 all-reduce.9
  111.9 73.9 all-reduce.11
  270.8 68.6 all-reduce.13
  510.2 65.0 all-reduce.15
  576.9 39.1 all-gather.8
  618.5 58.7 all-gather.6
where the time goes:
time: 777 us; the launch traced here: 776 us
  blocking collectives  346 us (45%)
  waiting for transfers between devices  329 us (42%)
  starting transfers between devices  31.2 us (4%)
  matrix products  26.7 us (3%)
  between operations  16.9 us (2%)
  local copies, waits for them, and re-layouts  16 us (2%)
  other arithmetic  9.93 us (1%)
    unnamed x2, blocking collectives  86.2 us
    psum x1, blocking collectives, local(): totals, picked = lax.psum((totals, picked), ('kv', 'seq', 'vocab'))  76.6 us
    psum x1, waiting for transfers between devices, local(): lax.psum((numerator, jnp.sum(weights, axis=-1)), 'seq')  73.8 us
    psum x1, waiting for transfers between devices, local(): lifted = lax.psum(lifted.astype(jnp.bfloat16), 'seq').astype(jnp.float32)  64.1 us
    psum x1, waiting for transfers between devices, local(): gate_up, ffn_squares = lax.psum((gate_up, ffn_squares), 'seq')  57.1 us
    all_gather x1, waiting for transfers between devices, local(): lax.all_gather(branch, ('kv', 'vocab'), axis=2, tiled=True)  52.4 us
    psum x1, waiting for transfers between devices, local(): lax.psum((projected_rows, jnp.sum(tenant_float * tenant_float, axis=-1)),...  50.6 us
    all_gather x1, blocking collectives, local(): gathered = lax.all_gather(normed, ('kv', 'vocab'), axis=0, tiled=True)  48.2 us
  transfers between devices with their start and end apart: 16, of which 6 were waited for; matrix products, arithmetic and copies ran while one was open for 3% of the time, Pallas kernels for 0%

commit v1 on v0

v1 whole, which is shorter than its diff:
```python
import jax
import jax.numpy as jnp
import numpy as np
from jax import lax
from jax.experimental import pallas as pl
from jax.experimental.pallas import tpu as pltpu
from jax.sharding import PartitionSpec as P

MESH = pl.DeviceIdType.MESH
F32 = jnp.float32
BF16 = jnp.bfloat16
WIDTH = 3584
EPSILON = 1e-06
SCORE_CAP = 50.0
LOGIT_CAP = 30.0
NT = (((1,), (1,)), ((), ()))


def rem(a, n):
    return lax.rem(a, jnp.int32(n))


def div(a, n):
    return lax.div(a, jnp.int32(n))


def dot(a, b):
    return jnp.dot(a, b, preferred_element_type=F32)


def dot_nt(a, b):
    return lax.dot_general(a, b, NT, preferred_element_type=F32)


def iota(shape, dim):
    return lax.broadcasted_iota(jnp.int32, shape, dim)


def send(src, dst, ssem, rsem, peer):
    pltpu.make_async_remote_copy(
        src_ref=src,
        dst_ref=dst,
        send_sem=ssem,
        recv_sem=rsem,
        device_id=peer,
        device_id_type=MESH,
    ).start()


def wait_bytes(ref, sem):
    pltpu.make_async_copy(ref, ref, sem).wait()


def plane_peer(p, d):
    q = rem(p + d, 32)
    return q, {"kv": div(q, 4), "vocab": rem(q, 4)}


def position_in_mesh():
    return lax.axis_index("kv"), lax.axis_index("seq"), lax.axis_index("vocab")


def project_kernel(
    h_ref, w_hbm, g_ref, anc_ref, len_ref, freq_ref, p48_ref,
    q_ref, k_ref, v_ref,
    w, pad8, xg, xf, ps, prc, sqs, sqr, agc, wsem, ssem, rsem,
):
    kv, z, _ = position_in_mesh()
    load = pltpu.make_async_copy(w_hbm, w, wsem)
    load.start()
    barrier = pltpu.get_barrier_semaphore()
    for d in range(1, 8):
        pl.semaphore_signal(barrier, inc=1, device_id={"kv": rem(kv + d, 8)}, device_id_type=MESH)
        pl.semaphore_signal(barrier, inc=1, device_id={"seq": rem(z + d, 8)}, device_id_type=MESH)
    pad8[...] = jnp.zeros_like(pad8)
    pad8[0:6, :] = h_ref[...].astype(F32)
    xg[kv] = pad8[...].astype(BF16)
    pl.semaphore_wait(barrier, 14)
    for d in range(1, 8):
        send(xg.at[kv], xg.at[kv], ssem.at[0], rsem.at[0], {"kv": rem(kv + d, 8)})
    depth = jnp.sum(anc_ref[...].astype(F32), axis=1, keepdims=True) - 1.0
    angle = (len_ref[0].astype(F32) + depth) * freq_ref[...]
    cosine = jnp.cos(angle)
    sine = jnp.sin(angle)
    load.wait()
    wait_bytes(xg.at[0:7], rsem.at[0])
    for j in range(8):
        xf[8 * j : 8 * j + 8, :] = xg[j].astype(F32)
    x = dot(p48_ref[...], xf[...].astype(BF16))
    eye = iota((48, 128), 0) == iota((48, 128), 1)
    squares = jnp.sum(x * x, axis=1, keepdims=True)
    row = jnp.sum(jnp.where(eye, squares, 0.0), axis=0, keepdims=True)
    sqs[...] = jnp.broadcast_to(row, (8, 128))
    part = dot((x * g_ref[...]).astype(BF16), w[...])
    for j in range(8):
        ps[j] = part[:, 128 * j : 128 * j + 128].astype(BF16)
    for d in range(1, 8):
        other = rem(z + d, 8)
        send(ps.at[other], prc.at[d - 1], ssem.at[1], rsem.at[1], {"seq": other})
        send(sqs, sqr.at[d - 1], ssem.at[2], rsem.at[2], {"seq": other})
    wait_bytes(sqr, rsem.at[2])
    total = sqs[...]
    for j in range(7):
        total = total + sqr[j]
    column = jnp.sum(jnp.where(eye, total[0:1, :], 0.0), axis=1, keepdims=True)
    inverse = lax.rsqrt(column / WIDTH + EPSILON)
    wait_bytes(prc, rsem.at[1])
    chunk = ps[z].astype(F32)
    for j in range(7):
        chunk = chunk + prc[j].astype(F32)
    agc[z] = (chunk * inverse).astype(BF16)
    for d in range(1, 8):
        send(agc.at[z], agc.at[z], ssem.at[3], rsem.at[3], {"seq": rem(z + d, 8)})
    wait_bytes(agc.at[0:7], rsem.at[3])
    for j, (ref, row0) in enumerate(((q_ref, 0), (q_ref, 48), (k_ref, 0))):
        first = agc[2 * j].astype(F32)
        second = agc[2 * j + 1].astype(F32)
        ref[row0 : row0 + 48, 0:128] = (first * cosine - second * sine).astype(BF16)
        ref[row0 : row0 + 48, 128:256] = (second * cosine + first * sine).astype(BF16)
    v_ref[:, 0:128] = agc[6]
    v_ref[:, 128:256] = agc[7]
    wait_bytes(xg.at[0:7], ssem.at[0])
    wait_bytes(prc, ssem.at[1])
    wait_bytes(sqr, ssem.at[2])
    wait_bytes(agc.at[0:7], ssem.at[3])


def capped_weight(scores):
    return jnp.exp(SCORE_CAP * jnp.tanh(scores * (0.0625 / SCORE_CAP)))


def attend_kernel(
    len_ref, path_ref, q_ref, kn_ref, vn_ref, anc_ref, keys_ref, values_ref,
    keys_out, values_out, num_out, den_out,
    num, den,
):
    step = pl.program_id(0)
    rows = keys_ref.shape[0]
    z = lax.axis_index("seq")
    length = len_ref[0]
    start = z * (rows * pl.num_programs(0)) + step * rows

    @pl.when(step == 0)
    def _():
        num[...] = jnp.zeros_like(num)
        den[...] = jnp.zeros_like(den)

    keys = keys_ref[...]
    values = values_ref[...]
    keys_out[...] = keys
    values_out[...] = values

    @pl.when((start + rows > length) & (start < length + 5))
    def _():
        away = start + iota((rows, 1), 0) - length
        target = jnp.full((rows, 1), -1, jnp.int32)
        for a in range(5):
            target = jnp.where(away == a, path_ref[0, a], target)
        selector = jnp.where(iota((rows, 48), 1) == target, 1.0, 0.0).astype(BF16)
        inside = jnp.broadcast_to(target, (rows, 256)) >= 0
        for fresh, old, out in ((kn_ref, keys, keys_out), (vn_ref, values, values_out)):
            out[...] = jnp.where(inside, dot(selector, fresh[...]), old.astype(F32)).astype(BF16)

    @pl.when(start < length)
    def _():
        weights = capped_weight(dot_nt(q_ref[...], keys))
        filled = iota((96, rows), 1) < length - start
        weights = jnp.where(filled, weights, 0.0)
        den[...] += jnp.sum(weights, axis=1, keepdims=True)
        num[...] += dot(weights.astype(BF16), values)

    @pl.when(step == pl.num_programs(0) - 1)
    def _():
        anc = jnp.where(z == 0, anc_ref[...], 0)
        for g in range(2):
            block = slice(48 * g, 48 * g + 48)
            weights = capped_weight(dot_nt(q_ref[block, :], kn_ref[...]))
            weights = jnp.where(anc > 0, weights, 0.0)
            den[block, :] += jnp.sum(weights, axis=1, keepdims=True)
            num[block, :] += dot(weights.astype(BF16), vn_ref[...])
        for j in range(8):
            num_out[j] = num[
                24 * (j // 2) : 24 * (j // 2) + 24, 128 * (j % 2) : 128 * (j % 2) + 128
            ].astype(BF16)
        eye = iota((96, 128), 0) == iota((96, 128), 1)
        row = jnp.sum(jnp.where(eye, den[...], 0.0), axis=0, keepdims=True)
        den_out[...] = jnp.broadcast_to(row, (8, 128))


def moments(values):
    lane = iota((8, 128), 1)
    tile = jnp.zeros((8, 128), F32)
    for i, v in enumerate(values):
        tile = jnp.where(lane == i, jnp.sum(v, axis=1, keepdims=True), tile)
    return tile


def finish_kernel(
    num_ref, den_ref, h_ref, wo_ref, gpa_ref, gpf_ref, gqf_ref, gfin_ref,
    wgu_hbm, wdown_hbm, wdraft_hbm, bias_ref, vocab_hbm, cand_ref,
    e64_ref, p192_ref, e256_ref, p96_ref,
    logn_ref, pick_ref,
    wgu, wdown, wdraft, wv, wp,
    nr, dr, ga, af, os_, orr, pad8, ms, mr, fp, xf, gs, gr, ags, acts, ds, dsr, ms2, mr2,
    npl, nz, nzs, nbo, nb, lf, dsl, dslr, bias, zb, bf, bs, big, basef, bbase, base4, tokb, tokd,
    rz, rzr, rp, accb, accd,
    wsem, ssem, rsem,
):
    kv, z, y = position_in_mesh()
    core = rem(kv, 2)
    p = kv * 4 + y
    loads = [
        pltpu.make_async_copy(wgu_hbm, wgu, wsem.at[0]),
        pltpu.make_async_copy(wdown_hbm, wdown, wsem.at[1]),
        pltpu.make_async_copy(wdraft_hbm, wdraft, wsem.at[2]),
        pltpu.make_async_copy(vocab_hbm, wv, wsem.at[3]),
    ]
    for load in loads:
        load.start()
    barrier = pltpu.get_barrier_semaphore()
    for d in range(1, 8):
        pl.semaphore_signal(barrier, inc=1, device_id={"seq": rem(z + d, 8)}, device_id_type=MESH)

    @pl.loop(1, 32)
    def _(d):
        pl.semaphore_signal(barrier, inc=1, device_id=plane_peer(p, d)[1], device_id_type=MESH)

    pl.semaphore_wait(barrier, 38)

    def to_seq(src, dst, s):
        for d in range(1, 8):
            other = rem(z + d, 8)
            send(src(other), dst(d), ssem.at[s], rsem.at[s], {"seq": other})

    def to_plane(src, dst, s):
        @pl.loop(1, 32)
        def _(d):
            q, peer = plane_peer(p, d)
            send(src(q), dst(d), ssem.at[s], rsem.at[s], peer)

    to_seq(lambda o: num_ref.at[o], lambda d: nr.at[d - 1], 0)
    to_seq(lambda o: den_ref, lambda d: dr.at[d - 1], 1)
    pad8[...] = jnp.zeros_like(pad8)
    pad8[0:6, :] = h_ref[...].astype(F32)
    wait_bytes(dr, rsem.at[1])
    total = den_ref[...]
    for j in range(7):
        total = total + dr[j]
    pick_lane = iota((24, 128), 1) == iota((24, 128), 0) + 24 * div(z, 2)
    den = jnp.sum(jnp.where(pick_lane, total[0:1, :], 0.0), axis=1, keepdims=True)
    wait_bytes(nr, rsem.at[0])
    num = num_ref[z].astype(F32)
    for j in range(7):
        num = num + nr[j].astype(F32)
    ga[z] = (num / den).astype(BF16)
    to_seq(lambda o: ga.at[z], lambda d: ga.at[z], 2)
    wait_bytes(ga.at[0:7], rsem.at[2])
    for j in range(8):
        r0, c0 = 24 * ((j // 2) % 2), 256 * (j // 4) + 128 * (j % 2)
        af[r0 : r0 + 24, c0 : c0 + 128] = ga[j].astype(F32)
    attended = dot(e64_ref[...], af[...].astype(BF16)).astype(BF16)
    out = dot_nt(attended, wo_ref[...])
    for j in range(8):
        os_[j] = out[8 * j : 8 * j + 8, :].astype(BF16)
    for d in range(1, 8):
        other = rem(kv + d, 8)
        send(os_.at[other], orr.at[d - 1], ssem.at[3], rsem.at[3], {"kv": other})
    hidden = pad8[...]
    wait_bytes(orr, rsem.at[3])
    att = os_[kv].astype(F32)
    for j in range(7):
        att = att + orr[j].astype(F32)
    gained = att * gpa_ref[...]
    ms[...] = moments((att * att, hidden * gained, gained * gained, hidden * hidden))
    to_seq(lambda o: ms, lambda d: mr.at[d - 1], 4)
    wait_bytes(mr, rsem.at[4])
    tot = ms[...]
    for j in range(7):
        tot = tot + mr[j]
    inv = lax.rsqrt(tot[:, 0:1] / WIDTH + EPSILON)
    first = (hidden + gained * inv).astype(BF16).astype(F32)
    square = tot[:, 3:4] + 2.0 * inv * tot[:, 1:2] + inv * inv * tot[:, 2:3]
    inv = lax.rsqrt(jnp.maximum(square, 0.0) / WIDTH + EPSILON)
    fp[p] = (first * inv * gpf_ref[...]).astype(BF16)
    to_plane(lambda q: fp.at[p], lambda d: fp.at[p], 5)
    loads[0].wait()
    wait_bytes(fp.at[0:31], rsem.at[5])
    for j in range(32):
        xf[8 * j : 8 * j + 8, :] = fp[j].astype(F32)
    x = dot(p192_ref[...], xf[...].astype(BF16)).astype(BF16)
    gu = dot(x, wgu[...])
    for j in range(8):
        gs[j] = gu[24 * j : 24 * j + 24, :].astype(BF16)
    to_seq(lambda o: gs.at[o], lambda d: gr.at[d - 1], 6)
    loads[1].wait()
    wait_bytes(gr, rsem.at[6])
    gu = gs[z].astype(F32)
    for j in range(7):
        gu = gu + gr[j].astype(F32)
    gate, up = gu[:, 0:448], gu[:, 448:896]
    gelu = 0.5 * gate * (1.0 + jnp.tanh(0.7978845608028654 * (gate + 0.044715 * gate * gate * gate)))
    ags[z] = (gelu * up).astype(BF16)
    to_seq(lambda o: ags.at[z], lambda d: ags.at[z], 7)
    wait_bytes(ags.at[0:7], rsem.at[7])
    for j in range(8):
        acts[24 * j : 24 * j + 24, :] = ags[j].astype(F32)
    act = dot(e256_ref[...], acts[...].astype(BF16)).astype(BF16)
    out = dot(act, wdown[...])
    for j in range(32):
        ds[j] = out[8 * j : 8 * j + 8, :].astype(BF16)
    to_plane(lambda q: ds.at[q], lambda d: dsr.at[d - 1], 8)
    loads[2].wait()
    loads[3].wait()
    spread = iota((896, 1024), 0) == (lax.shift_right_logical(iota((896, 1024), 1), 7) * 112 + (iota((896, 1024), 1) & 127))
    spread = jnp.where(spread & ((iota((896, 1024), 1) & 127) < 112), 1.0, 0.0).astype(BF16)
    for j in range(4):
        wp[0:512, 1024 * j : 1024 * j + 1024] = dot(
            wv[:, 896 * j : 896 * j + 896], spread
        ).astype(BF16)
    send(wp.at[0:512], wp.at[512:1024], ssem.at[9], rsem.at[9], {"kv": kv + 1 - 2 * core})
    wait_bytes(dsr, rsem.at[8])
    out = ds[p].astype(F32)
    for j in range(31):
        out = out + dsr[j].astype(F32)
    gained = out * gqf_ref[...]
    ms2[...] = moments((out * out, first * gained, gained * gained, first * first))
    to_seq(lambda o: ms2, lambda d: mr2.at[d - 1], 10)
    lf[...] = jnp.zeros_like(lf)
    bias[...] = jnp.zeros_like(bias)
    bias[0:4, 0:112] = bias_ref[...]
    wait_bytes(mr2, rsem.at[10])
    tot = ms2[...]
    for j in range(7):
        tot = tot + mr2[j]
    inv = lax.rsqrt(tot[:, 0:1] / WIDTH + EPSILON)
    second = (first + gained * inv).astype(BF16).astype(F32)
    square = tot[:, 3:4] + 2.0 * inv * tot[:, 1:2] + inv * inv * tot[:, 2:3]
    inv = lax.rsqrt(jnp.maximum(square, 0.0) / WIDTH + EPSILON)
    normed = (second * inv * gfin_ref[...]).astype(BF16)
    npl[p] = normed
    to_plane(lambda q: npl.at[p], lambda d: npl.at[p], 11)
    nz[z] = dot(normed, spread[0:448, 0:512]).astype(BF16)
    to_seq(lambda o: nz.at[z], lambda d: nz.at[z], 12)
    wait_bytes(npl.at[0:31], rsem.at[11])
    for j in range(32):
        xf[8 * j : 8 * j + 8, :] = npl[j].astype(F32)
    x = dot(p192_ref[...], xf[...].astype(BF16)).astype(BF16)
    for i in range(4):
        lf[i, :, 0:112] = dot(x, wdraft[i])
    for j in range(8):
        for i in range(4):
            dsl[j, i] = lf[i, 24 * j : 24 * j + 24, :].astype(BF16)
    to_seq(lambda o: dsl.at[o], lambda d: dslr.at[d - 1], 13)
    wait_bytes(nz.at[0:7], rsem.at[12])
    for j in range(8):
        nzs[:, 512 * j : 512 * j + 512] = nz[j].astype(F32)
    half = div(y, 2)
    slot = kv * 2 + rem(y, 2)
    nbo[...] = nzs[...].astype(BF16)

    @pl.loop(0, 16)
    def _(d):
        q = rem(div(kv, 2) * 4 + y + d, 16)
        target = 2 * div(q, 4) + half
        to_me = (d == 0) & (half == core)

        @pl.when(jnp.logical_not(to_me))
        def _():
            send(nbo, nb.at[slot], ssem.at[14], rsem.at[14], {"kv": target, "vocab": rem(q, 4)})

        @pl.when(to_me)
        def _():
            pltpu.make_async_copy(nbo, nb.at[slot], rsem.at[14]).start()

    wait_bytes(dslr, rsem.at[13])
    for i in range(4):
        lifted = dsl[z, i].astype(F32)
        for j in range(7):
            lifted = lifted + dslr[j, i].astype(F32)
        lifted = lifted + bias[i : i + 1, :]
        zb[z, i] = (lifted / (1.0 + jnp.exp(-lifted))).astype(BF16)
    to_seq(lambda o: zb.at[z], lambda d: zb.at[z], 15)
    wait_bytes(zb.at[0:7], rsem.at[15])
    for j in range(8):
        for i in range(4):
            bf[i, 24 * j : 24 * j + 24, :] = zb[j, i].astype(F32)
    for i in range(4):
        for hf in range(2):
            bs[hf, i] = bf[i, 96 * hf : 96 * hf + 96, :].astype(BF16)
    columns = pl.ds(pl.multiple_of(p * 128, 128), 128)

    @pl.loop(1, 32)
    def _(d):
        q, peer = plane_peer(p, d)
        send(bs.at[rem(div(q, 4), 2)], big.at[:, :, columns], ssem.at[16], rsem.at[16], peer)

    for i in range(4):
        big[i, :, columns] = bs[core, i]
    for n in range(5):
        for k in range(2):
            tokens = cand_ref[n, 2 * core + k]
            if n == 0:
                tokb[:, 48 * k : 48 * k + 48] = tokens
            else:
                lane = 96 * (n - 1) + 48 * k
                tokd[:, lane : lane + 48] = tokens
    linear = (kv * 8 + z) * 4 + y
    sibling = ((kv + 1 - 2 * core) * 8 + z) * 4 + y
    accb[...] = jnp.zeros_like(accb)
    accd[...] = jnp.zeros_like(accd)

    def score(raw, tokens, acc, lanes, first_id):
        logits = LOGIT_CAP * jnp.tanh(raw * (1.0 / LOGIT_CAP))
        where = iota(raw.shape, 0)
        local = tokens - first_id
        for c in range(8):
            hit = where == local[c : c + 1, :]
            acc[c : c + 1, 0:lanes] += jnp.sum(jnp.where(hit, logits, 0.0), axis=0, keepdims=True)
        acc[8:9, 0:lanes] += jnp.sum(jnp.exp(logits), axis=0, keepdims=True)

    def first_id(i):
        return jnp.where(i < 2, linear * 512 + 256 * i, sibling * 512 + 256 * (i - 2))

    wait_bytes(nb, rsem.at[14])
    for t in range(16):
        basef[8 * t : 8 * t + 8, :] = nb[t].astype(F32)
    bbase[...] = dot(p96_ref[...], basef[...].astype(BF16)).astype(BF16)
    wait_bytes(wp.at[0:512], rsem.at[9])

    @pl.loop(0, 4)
    def _(i):
        rows = pl.ds(pl.multiple_of(i * 256, 256), 256)
        raw = dot_nt(wp[rows, :], bbase[...])
        for d in range(4):
            base4[rows, 96 * d : 96 * d + 96] = raw
        score(raw, tokb[:, 0:96], accb, 96, first_id(i))

    wait_bytes(big.at[:, :, 0:3968], rsem.at[16])

    @pl.loop(0, 4)
    def _(i):
        rows = pl.ds(pl.multiple_of(i * 256, 256), 256)
        raw = dot_nt(wp[rows, :], big[...].reshape(384, 4096)) + base4[rows, :]
        score(raw, tokd[...], accd, 384, first_id(i))

    rz[:, 0:128] = accb[...].astype(BF16)
    rz[:, 128:512] = accd[...].astype(BF16)
    to_seq(lambda o: rz, lambda d: rzr.at[d - 1], 17)
    wait_bytes(rzr, rsem.at[17])
    res = rz[...].astype(F32)
    for j in range(7):
        res = res + rzr[j].astype(F32)
    rp[p] = res.astype(BF16)
    to_plane(lambda q: rp.at[p], lambda d: rp.at[p], 18)
    wait_bytes(rp.at[0:31], rsem.at[18])
    for c in range(2):
        res = jnp.zeros((16, 512), F32)
        for x4 in range(4):
            for yy in range(4):
                res = res + rp[(2 * x4 + c) * 4 + yy].astype(F32)
        logs = jnp.log(res[8:9, :])
        for n in range(5):
            for k in range(2):
                lane = 48 * k if n == 0 else 128 + 96 * (n - 1) + 48 * k
                logn_ref[n, 2 * c + k : 2 * c + k + 1, :] = logs[:, lane : lane + 48]
                pick_ref[n, 2 * c + k] = res[0:8, lane : lane + 48]

    for s, ref in (
        (0, nr), (1, dr), (2, ga.at[0:7]), (3, orr), (4, mr), (5, fp.at[0:31]), (6, gr),
        (7, ags.at[0:7]), (8, dsr), (9, wp.at[0:512]), (10, mr2), (11, npl.at[0:31]),
        (12, nz.at[0:7]), (13, dslr), (14, nb.at[0:15]), (15, zb.at[0:7]),
        (16, big.at[:, :, 0:3968]), (17, rzr), (18, rp.at[0:31]),
    ):
        wait_bytes(ref, ssem.at[s])

    @pl.when(half != core)
    def _():
        wait_bytes(nbo, ssem.at[14])


def one_hot_rows(rows, columns, places):
    table = np.zeros((rows, columns), np.float32)
    table[np.arange(rows), places] = 1.0
    return table


def tables():
    r48 = np.arange(48)
    p48 = one_hot_rows(48, 64, (r48 // 6) * 8 + r48 % 6)
    r192 = np.arange(192)
    tenant, node = r192 // 48, r192 % 48
    p192 = one_hot_rows(192, 256, ((node // 6) * 4 + tenant) * 8 + node % 6)
    r96 = np.arange(96)
    tenant, node = r96 // 48, r96 % 48
    p96 = one_hot_rows(96, 128, ((node // 6) * 2 + tenant) * 8 + node % 6)
    return p48, p192, p96


def vmem(shape, dtype=BF16):
    return pltpu.VMEM(shape, dtype)


VM = pl.BlockSpec(memory_space=pltpu.VMEM)
SM = pl.BlockSpec(memory_space=pltpu.SMEM)
ANY = pl.BlockSpec(memory_space=pl.ANY)
DMA = pltpu.SemaphoreType.DMA


def local(
    hidden_state,
    input_projection,
    output_projection,
    norm_pre_attention,
    norm_post_attention,
    norm_pre_feedforward,
    norm_post_feedforward,
    norm_final,
    cache_keys,
    cache_values,
    cache_length,
    ancestors,
    accepted_path,
    gate_up_weight,
    down_weight,
    draft_weight,
    draft_bias,
    vocab_weight,
    candidate_tokens,
):
    p48, p192, p96 = (jnp.asarray(t, BF16) for t in tables())
    e64, e256 = p48.T, p192.T
    frequency = 10000.0 ** (-2.0 * jnp.arange(128, dtype=F32) / 256)
    own = hidden_state.reshape(6, 448)
    anc = ancestors[0]
    queries, new_keys, new_values = pl.pallas_call(
        project_kernel,
        name="project",
        out_shape=(
            jax.ShapeDtypeStruct((96, 256), BF16),
            jax.ShapeDtypeStruct((48, 256), BF16),
            jax.ShapeDtypeStruct((48, 256), BF16),
        ),
        in_specs=[VM, ANY, VM, VM, SM, VM, VM],
        out_specs=(VM, VM, VM),
        scratch_shapes=[
            vmem((448, 1024)), vmem((8, 448), F32), vmem((8, 8, 448)), vmem((64, 448), F32),
            vmem((8, 48, 128)), vmem((7, 48, 128)), vmem((8, 128), F32), vmem((7, 8, 128), F32),
            vmem((8, 48, 128)), DMA, DMA((4,)), DMA((4,)),
        ],
        compiler_params=pltpu.CompilerParams(
            collective_id=0, has_side_effects=True, vmem_limit_bytes=32 << 20
        ),
    )(
        own, input_projection.reshape(448, 1024), norm_pre_attention.reshape(1, 448), anc,
        cache_length, frequency.reshape(1, 128), p48,
    )
    slots = cache_keys.shape[1]
    block = 512
    rowspec = pl.BlockSpec((block, 256), lambda i: (i, 0))

    def whole(shape):
        return pl.BlockSpec(shape, lambda i: (0,) * len(shape))

    keys_updated, values_updated, numerators, denominators = pl.pallas_call(
        attend_kernel,
        name="attend",
        grid=(slots // block,),
        out_shape=(
            jax.ShapeDtypeStruct((slots, 256), BF16),
            jax.ShapeDtypeStruct((slots, 256), BF16),
            jax.ShapeDtypeStruct((8, 24, 128), BF16),
            jax.ShapeDtypeStruct((8, 128), F32),
        ),
        in_specs=[
            SM, SM, whole((96, 256)), whole((48, 256)), whole((48, 256)), whole((48, 48)),
            rowspec, rowspec,
        ],
        out_specs=(rowspec, rowspec, whole((8, 24, 128)), whole((8, 128))),
        scratch_shapes=[vmem((96, 256), F32), vmem((96, 1), F32)],
        compiler_params=pltpu.CompilerParams(vmem_limit_bytes=32 << 20),
    )(
        cache_length, accepted_path, queries, new_keys, new_values, anc,
        cache_keys.reshape(slots, 256), cache_values.reshape(slots, 256),
    )
    log_normalizer, picked = pl.pallas_call(
        finish_kernel,
        name="finish",
        out_shape=(
            jax.ShapeDtypeStruct((5, 4, 48), F32),
            jax.ShapeDtypeStruct((5, 4, 8, 48), F32),
        ),
        in_specs=[VM] * 8 + [ANY] * 3 + [VM, ANY] + [VM] * 5,
        out_specs=(VM, VM),
        scratch_shapes=[
            vmem((448, 896)), vmem((448, 448)), vmem((4, 448, 112)), vmem((512, 3584)),
            vmem((1024, 4096)),
            vmem((7, 24, 128)), vmem((7, 8, 128), F32), vmem((8, 24, 128)), vmem((48, 512), F32),
            vmem((8, 8, 448)), vmem((7, 8, 448)), vmem((8, 448), F32),
            vmem((8, 128), F32), vmem((7, 8, 128), F32), vmem((32, 8, 448)), vmem((256, 448), F32),
            vmem((8, 24, 896)), vmem((7, 24, 896)), vmem((8, 24, 448)), vmem((192, 448), F32),
            vmem((32, 8, 448)), vmem((31, 8, 448)), vmem((8, 128), F32), vmem((7, 8, 128), F32),
            vmem((32, 8, 448)), vmem((8, 8, 512)), vmem((8, 4096), F32), vmem((8, 4096)),
            vmem((16, 8, 4096)),
            vmem((4, 192, 128), F32), vmem((8, 4, 24, 128)), vmem((7, 4, 24, 128)),
            vmem((8, 128), F32), vmem((8, 4, 24, 128)), vmem((4, 192, 128), F32),
            vmem((2, 4, 96, 128)), vmem((4, 96, 4096)), vmem((128, 4096), F32), vmem((96, 4096)),
            vmem((1024, 384), F32), vmem((8, 128), jnp.int32), vmem((8, 384), jnp.int32),
            vmem((16, 512)), vmem((7, 16, 512)), vmem((32, 16, 512)),
            vmem((16, 128), F32), vmem((16, 384), F32),
            DMA((4,)), DMA((19,)), DMA((19,)),
        ],
        compiler_params=pltpu.CompilerParams(
            collective_id=1, has_side_effects=True, vmem_limit_bytes=60 << 20
        ),
    )(
        numerators, denominators, own, output_projection[0].T,
        norm_post_attention.reshape(1, 448), norm_pre_feedforward.reshape(1, 448),
        norm_post_feedforward.reshape(1, 448), norm_final.reshape(1, 448),
        gate_up_weight.reshape(448, 896), down_weight, draft_weight, draft_bias, vocab_weight,
        jnp.transpose(candidate_tokens, (0, 2, 3, 1)), e64, p192, e256, p96,
    )
    return (
        keys_updated.reshape(cache_keys.shape),
        values_updated.reshape(cache_values.shape),
        jnp.transpose(log_normalizer, (0, 2, 1)),
        jnp.transpose(picked, (0, 3, 1, 2)),
    )


def solution(mesh):
    placed = (
        P("kv", "vocab", "seq"),
        P("seq", "kv", None),
        P("kv", None, "seq"),
        P("seq"),
        P("seq"),
        P("seq"),
        P("seq"),
        P("seq"),
        P("vocab", "seq", "kv", None),
        P("vocab", "seq", "kv", None),
        P("vocab"),
        P("vocab", None, None),
        P("vocab", None),
        P("seq", None, ("kv", "vocab")),
        P(("kv", "vocab"), "seq"),
        P(None, "seq", ("kv", "vocab")),
        P(None, ("kv", "vocab")),
        P(("kv", "seq", "vocab"), None),
        P(),
    )
    return jax.shard_map(
        local,
        mesh=mesh,
        in_specs=placed,
        out_specs=(P("vocab", "seq", "kv", None), P("vocab", "seq", "kv", None), P(), P()),
        check_vma=False,
    )
```

time: 777 us -> 204 us (0.26)
  blocking collectives: 346 us -> 0 us
  waiting for transfers between devices: 329 us -> 0 us
  Pallas kernels: 0 us -> 188 us
  starting transfers between devices: 31.2 us -> 0 us
  matrix products: 26.7 us -> 0 us
  between operations: 16.9 us -> 1.33 us
  other arithmetic: 9.93 us -> 0.01 us
    psum x4 -> x0, waiting for transfers between devices: 246 us -> none  [the longest x1 73.8 us: local(): lax.psum((numerator, jnp.sum(weights, axis=-1)), 'seq')]
    pallas_call x0 -> x3, Pallas kernels: none -> 188 us  [the longest x1 160 us: local(): pl.pallas_call(finish_kernel, name='finish', out_shape=(jax.ShapeDtypeStr...]
    psum x7 -> x0, blocking collectives: 151 us -> none  [the longest x1 76.6 us: local(): totals, picked = lax.psum((totals, picked), ('kv', 'seq', 'vocab'))]
    all_gather x3 -> x0, blocking collectives: 110 us -> none  [the longest x1 48.2 us: local(): gathered = lax.all_gather(normed, ('kv', 'vocab'), axis=0, tiled=True)]
    unnamed x2 -> x0, blocking collectives: 86.2 us -> none
    all_gather x2 -> x0, waiting for transfers between devices: 82.9 us -> none  [the longest x1 52.4 us: local(): lax.all_gather(branch, ('kv', 'vocab'), axis=2, tiled=True)]
    unnamed x10 -> x0, starting transfers between devices: 30.7 us -> none
    dot_general x13 -> x0, matrix products: 26.7 us -> none  [the longest x1 8.23 us: local(): jnp.einsum('tnc,vc->tnv', lax.all_gather(branch, ('kv', 'vocab'), axis=2,...]
  transfers between devices with their start and end apart: 16 -> 0, of which waited for: 6 -> 0; matrix products, arithmetic and copies ran while one was open for 3% -> 0% of each run, Pallas kernels for 0% -> 0%
where the time goes in v1:
time: 204 us; the launch traced here: 203 us
  Pallas kernels  188 us (92%)
  local copies, waits for them, and re-layouts  13.5 us (7%)
    pallas_call x1, Pallas kernels, local(): pl.pallas_call(finish_kernel, name='finish', out_shape=(jax.ShapeDtypeStr...  160 us
    pallas_call x1, Pallas kernels, local(): pl.pallas_call(project_kernel, name='project', out_shape=(jax.ShapeDtypeS...  24.1 us
    unnamed x26, local copies, waits for them, and re-layouts  11.9 us

profile of v1, /device:TPU:1, one launch (start us, length us, event | category | flops | bytes accessed | tf_op | source)
XLA Modules:
  0.0 203.3 jit_solution(3744243497562200485)
XLA Ops:
  1.3 0.0 copy-start.2
  1.3 1.2 copy-done.2
  2.5 0.0 copy-start.3
  2.5 0.7 copy-done.3
  3.2 0.0 copy-start.6
  3.2 0.7 copy-done.6
  3.9 0.0 copy-start.7
  3.9 0.7 copy-done.7
  4.6 0.0 copy-start.9
  4.6 0.7 copy-done.9
  5.3 0.0 copy-start.11
  5.3 24.1 %project.1 = (bf16[96,256]{1,0:T(8,128)(2,1)S(1)}, bf16[48,256]{1,0:T(8,128)(2,1)S(1)}, bf16[48,256]{1,0:T(8,128)(2,1)S(1)}) custom-call(bf16[6,448]{1,0:T(8,128)(2,1)S(1)} %bitcast.24, bf16[448,1024]{1,0:T(8,128)(2,1)S(1)} %bitcast.20, f32[1,448]{1,0:T(1,128)S(1)} %bitcast.25, s32[48,48]{1,0:T(8,128)S(1)} %bitcast.21, s32[1]{0:T(128)S(6)} %copy.28.len_ref, ...), custom_call_target="tpu_custom_call" | custom-call | tf_op jit(solution)/shard_map/project/pallas_call | solution.py:535
  29.4 0.0 copy-start
  29.4 1.2 copy-done
  30.6 0.0 copy-start.1
  30.6 1.2 copy-done.1
  31.8 0.0 copy-start.4
  31.8 0.7 copy-done.4
  32.6 0.0 copy-start.10
  32.6 0.7 copy-done.10
  33.2 4.0 %attend.1 = (bf16[2048,256]{1,0:T(8,128)(2,1)}, bf16[2048,256]{1,0:T(8,128)(2,1)}, bf16[8,24,128]{2,1,0:T(8,128)(2,1)S(1)}, f32[8,128]{1,0:T(8,128)S(1)}) custom-call(s32[1]{0:T(128)S(6)} %copy.28.len_ref, s32[1,5]{1,0:T(1,128)S(1)} %copy-done.10, bf16[96,256]{1,0:T(8,128)(2,1)S(1)} %get-tuple-element.13.q_ref, ...), custom_call_target="tpu_custom_call" | custom-call | tf_op jit(solution)/shard_map/attend/pallas_call | solution.py:564
  37.2 0.0 copy-start.5
  37.2 0.6 copy-done.5
  37.8 0.0 copy-start.8
  37.8 0.6 copy-done.8
  38.4 0.0 copy-done.11
  38.4 1.6 reshape.66.wgu_hbm
  40.0 160.4 %finish.1 = (f32[5,4,48]{2,1,0:T(4,128)}, f32[5,4,8,48]{3,2,1,0:T(8,128)}) custom-call(bf16[8,24,128]{2,1,0:T(8,128)(2,1)} %copy-done.5, f32[8,128]{1,0:T(8,128)} %copy-done.8, bf16[6,448]{1,0:T(8,128)(2,1)} %bitcast.23, bf16[448,512]{1,0:T(8,128)(2,1)} %bitcast.26, f32[1,448]{1,0:T(1,128)} %bitcast.30, f32[1,448]{1,0:T(1,128)} %bitcast.31, ...), custom_call_target="tpu_custom_call" | custom-call | tf_op jit(solution)/shard_map/finish/pallas_call | solution.py:585
  200.4 1.3 copy.29
  201.7 1.5 copy.30
  (1 shorter events, 0.0 us)
Async XLA Ops:
  1.3 1.2 copy-start.2
  2.5 0.7 copy-start.3
  3.2 0.7 copy-start.6
  3.9 0.7 copy-start.7
  4.6 0.7 copy-start.9
  5.3 33.1 %copy-start.11 = (bf16[448,2,448]{2,1,0:T(2,128)(2,1)S(1)}, bf16[448,2,448]{2,1,0:T(2,128)(2,1)}, u32[]{:S(2)}) copy-start(bf16[448,2,448]{2,1,0:T(2,128)(2,1)} %param.35) | copy-start | bytes 2408452
  29.4 1.2 copy-start
  30.6 1.2 copy-start.1
  31.8 0.7 copy-start.4
  32.6 0.7 copy-start.10
  37.2 0.6 copy-start.5
  37.8 0.6 copy-start.8

commit v2 on v0

v2 whole, which is shorter than its diff:
```python
import jax
import jax.numpy as jnp
import numpy as np
from jax import lax
from jax.experimental import pallas as pl
from jax.experimental.pallas import tpu as pltpu
from jax.sharding import PartitionSpec as P

MESH = pl.DeviceIdType.MESH
F32 = jnp.float32
BF16 = jnp.bfloat16
WIDTH = 3584
EPSILON = 1e-06
SCORE_CAP = 50.0
LOGIT_CAP = 30.0
NT = (((1,), (1,)), ((), ()))


def rem(a, n):
    return lax.rem(a, jnp.int32(n))


def div(a, n):
    return lax.div(a, jnp.int32(n))


def dot(a, b):
    return jnp.dot(a, b, preferred_element_type=F32)


def dot_nt(a, b):
    return lax.dot_general(a, b, NT, preferred_element_type=F32)


def iota(shape, dim):
    return lax.broadcasted_iota(jnp.int32, shape, dim)


def send(src, dst, ssem, rsem, peer):
    pltpu.make_async_remote_copy(
        src_ref=src,
        dst_ref=dst,
        send_sem=ssem,
        recv_sem=rsem,
        device_id=peer,
        device_id_type=MESH,
    ).start()


def wait_bytes(ref, sem):
    pltpu.make_async_copy(ref, ref, sem).wait()


def plane_peer(p, d):
    q = rem(p + d, 32)
    return q, {"kv": div(q, 4), "vocab": rem(q, 4)}


def position_in_mesh():
    return lax.axis_index("kv"), lax.axis_index("seq"), lax.axis_index("vocab")


def capped_weight(scores):
    return jnp.exp(SCORE_CAP * jnp.tanh(scores * (0.0625 / SCORE_CAP)))


def moments(values):
    lane = iota((8, 128), 1)
    tile = jnp.zeros((8, 128), F32)
    for i, v in enumerate(values):
        tile = jnp.where(lane == i, jnp.sum(v, axis=1, keepdims=True), tile)
    return tile


def rms_inverse(total):
    return lax.rsqrt(jnp.maximum(total, 0.0) / WIDTH + EPSILON)


LOADS = (
    "h", "p48", "g_att", "w_in", "freq", "anc", "keys", "values", "e64", "w_out", "g_post",
    "g_pre", "p192", "w_gu", "e256", "w_down", "g_fpost", "g_fin", "w_draft", "bias", "cand",
    "p96", "w_voc",
)


def step_kernel(len_ref, *refs):
    count = len(LOADS)
    source = dict(zip(LOADS, refs[:count]))
    kn, vn, res_ref = refs[count : count + 3]
    here = dict(zip(LOADS, refs[count + 3 : 2 * count + 3]))
    (
        wp, spread, pad8, xg, xf6, ps, prc, agc, qs,
        den, num, ns, nr, ga, af, os_, orr, ms, mr, fp, xf, gs, gr, ags, acts, ds, dsr,
        ms2, mr2, npl, nz, nzs, nbo, nb, lf, dsl, dslr, biasf, zbo, zb, bf, big, basef, bbase,
        base4, tokb, tokd, rz, rzr, rp, accb, accd,
        wsem, ssem, rsem, sring, r1, r2, r2h,
    ) = refs[2 * count + 3 :]
    kv, z, y = position_in_mesh()
    core = rem(kv, 2)
    x = div(kv, 2)
    p = kv * 4 + y
    sibling = kv + 1 - 2 * core
    copies = {}
    for i, name in enumerate(LOADS):
        copies[name] = pltpu.make_async_copy(source[name], here[name], wsem.at[i])
        copies[name].start()

    def get(name):
        copies[name].wait()
        return here[name]

    barrier = pltpu.get_barrier_semaphore()
    for d in range(1, 8):
        other = rem(z + d, 8)
        pl.semaphore_signal(barrier, inc=1, device_id={"seq": other}, device_id_type=MESH)
        pl.semaphore_signal(barrier, inc=1, device_id={"kv": sibling, "seq": other}, device_id_type=MESH)

    @pl.loop(1, 32)
    def _(d):
        pl.semaphore_signal(barrier, inc=1, device_id=plane_peer(p, d)[1], device_id_type=MESH)

    sent = []

    def to_seq(src, dst, s, total):
        for d in range(1, 8):
            other = rem(z + d, 8)
            send(src(other), dst(d), ssem.at[s], rsem.at[s], {"seq": other})
        sent.append((total, s))

    def to_kv(src, dst, s, total):
        for d in range(1, 8):
            other = rem(kv + d, 8)
            send(src(other), dst(d), ssem.at[s], rsem.at[s], {"kv": other})
        sent.append((total, s))

    def to_plane(src, dst, s, total):
        @pl.loop(1, 32)
        def _(d):
            q, peer = plane_peer(p, d)
            send(src(q), dst(d), ssem.at[s], rsem.at[s], peer)

        sent.append((total, s))

    pad8[...] = jnp.zeros_like(pad8)
    pad8[0:6, :] = get("h")[...].astype(F32)
    xg[kv] = pad8[...].astype(BF16)
    pl.semaphore_wait(barrier, 45)
    to_kv(lambda o: xg.at[kv], lambda d: xg.at[kv], 0, xg.at[0:7])
    depth = jnp.sum(get("anc")[...].astype(F32), axis=1, keepdims=True) - 1.0
    angle = (len_ref[0].astype(F32) + depth) * get("freq")[...]
    cosine = jnp.cos(angle)
    sine = jnp.sin(angle)
    eye = iota((96, 128), 0) == iota((96, 128), 1)
    p48 = get("p48")
    gain = get("g_att")[...]
    w_in = get("w_in")
    wait_bytes(xg.at[0:7], rsem.at[0])
    for j in range(8):
        xf6[8 * j : 8 * j + 8, :] = xg[j].astype(F32)
    tokens = dot(p48[...], xf6[...].astype(BF16))
    squares = jnp.sum(tokens * tokens, axis=1, keepdims=True)
    row = jnp.sum(jnp.where(eye[0:48], squares, 0.0), axis=0, keepdims=True)
    row = jnp.broadcast_to(row, (16, 128)).astype(BF16)
    part = dot((tokens * gain).astype(BF16), w_in[...])
    for j in range(8):
        ps[j, 0:48, :] = part[:, 128 * j : 128 * j + 128].astype(BF16)
        ps[j, 48:64, :] = row
    to_seq(lambda o: ps.at[o], lambda d: prc.at[d - 1], 1, prc)
    lane = iota((896, 1024), 1)
    inside = lane & 127
    place = lax.shift_right_logical(lane, 7) * 112 + inside
    spread[...] = jnp.where((iota((896, 1024), 0) == place) & (inside < 112), 1.0, 0.0).astype(BF16)
    wait_bytes(prc, rsem.at[1])
    chunk = ps[z].astype(F32)
    for j in range(7):
        chunk = chunk + prc[j].astype(F32)
    column = jnp.sum(jnp.where(eye[0:48], chunk[48:49, :], 0.0), axis=1, keepdims=True)
    agc[z] = (chunk[0:48] * rms_inverse(column)).astype(BF16)
    to_seq(lambda o: agc.at[z], lambda d: agc.at[z], 2, agc.at[0:7])
    keys, values = get("keys"), get("values")
    wait_bytes(agc.at[0:7], rsem.at[2])
    for j, (ref, row0) in enumerate(((qs, 0), (qs, 48), (kn, 0))):
        first = agc[2 * j].astype(F32)
        second = agc[2 * j + 1].astype(F32)
        ref[row0 : row0 + 48, 0:128] = (first * cosine - second * sine).astype(BF16)
        ref[row0 : row0 + 48, 128:256] = (second * cosine + first * sine).astype(BF16)
    vn[:, 0:128] = agc[6]
    vn[:, 128:256] = agc[7]

    queries = qs[...]
    anc = jnp.where(z == 0, here["anc"][...], 0)
    anc = jnp.concatenate([anc, anc], axis=0)
    weights = capped_weight(dot_nt(queries, kn[...]))
    weights = jnp.where(anc > 0, weights, 0.0)
    den[...] = jnp.sum(weights, axis=1, keepdims=True)
    num[...] = dot(weights.astype(BF16), vn[...])
    filled = len_ref[0] - z * 2048

    @pl.loop(0, 4)
    def _(i):
        rows = pl.ds(pl.multiple_of(i * 512, 512), 512)
        weights = capped_weight(dot_nt(queries, keys[rows, :]))
        weights = jnp.where(iota((96, 512), 1) < filled - i * 512, weights, 0.0)
        den[...] += jnp.sum(weights, axis=1, keepdims=True)
        num[...] += dot(weights.astype(BF16), values[rows, :])

    row = jnp.sum(jnp.where(eye, den[...], 0.0), axis=0, keepdims=True)
    row = jnp.broadcast_to(row, (16, 128)).astype(BF16)
    for j in range(8):
        r0, c0 = 24 * (j // 2), 128 * (j % 2)
        ns[j, 0:16, :] = row
        ns[j, 16:40, :] = num[r0 : r0 + 24, c0 : c0 + 128].astype(BF16)
    to_seq(lambda o: ns.at[o], lambda d: nr.at[d - 1], 3, nr)
    e64, w_out = get("e64"), get("w_out")
    wait_bytes(nr, rsem.at[3])
    total = ns[z].astype(F32)
    for j in range(7):
        total = total + nr[j].astype(F32)
    chosen = iota((24, 128), 1) == iota((24, 128), 0) + 24 * div(z, 2)
    below = jnp.sum(jnp.where(chosen, total[0:1, :], 0.0), axis=1, keepdims=True)
    ga[z] = (total[16:40, :] / below).astype(BF16)
    to_seq(lambda o: ga.at[z], lambda d: ga.at[z], 4, ga.at[0:7])
    w_voc = get("w_voc")

    def widen(j):
        wp[0:512, 1024 * j : 1024 * j + 1024] = dot(
            w_voc[:, 896 * j : 896 * j + 896], spread[...]
        ).astype(BF16)

    wait_bytes(ga.at[0:7], rsem.at[4])
    for j in range(8):
        r0, c0 = 24 * ((j // 2) % 2), 256 * (j // 4) + 128 * (j % 2)
        af[r0 : r0 + 24, c0 : c0 + 128] = ga[j].astype(F32)
    attended = dot(e64[...], af[...].astype(BF16)).astype(BF16)
    out = dot_nt(attended, w_out[...])
    for j in range(8):
        os_[j] = out[8 * j : 8 * j + 8, :].astype(BF16)
    to_kv(lambda o: os_.at[o], lambda d: orr.at[d - 1], 5, orr)
    hidden = pad8[...]
    gain = get("g_post")[...]
    wait_bytes(orr, rsem.at[5])
    att = os_[kv].astype(F32)
    for j in range(7):
        att = att + orr[j].astype(F32)
    gained = att * gain
    ms[...] = moments((att * att, hidden * gained, gained * gained, hidden * hidden))
    to_seq(lambda o: ms, lambda d: mr.at[d - 1], 6, mr)
    gain = get("g_pre")[...]
    wait_bytes(mr, rsem.at[6])
    tot = ms[...]
    for j in range(7):
        tot = tot + mr[j]
    inv = rms_inverse(tot[:, 0:1])
    first = (hidden + gained * inv).astype(BF16).astype(F32)
    inv = rms_inverse(tot[:, 3:4] + 2.0 * inv * tot[:, 1:2] + inv * inv * tot[:, 2:3])
    fp[p] = (first * inv * gain).astype(BF16)
    to_plane(lambda q: fp.at[p], lambda d: fp.at[p], 7, fp.at[0:31])
    widen(0)
    p192, w_gu = get("p192"), get("w_gu")
    wait_bytes(fp.at[0:31], rsem.at[7])
    for j in range(32):
        xf[8 * j : 8 * j + 8, :] = fp[j].astype(F32)
    rows192 = dot(p192[...], xf[...].astype(BF16)).astype(BF16)
    gu = dot(rows192, w_gu[...])
    for j in range(8):
        gs[j] = gu[24 * j : 24 * j + 24, :].astype(BF16)
    to_seq(lambda o: gs.at[o], lambda d: gr.at[d - 1], 8, gr)
    widen(1)
    widen(2)
    widen(3)
    send(wp.at[0:512], wp.at[512:1024], ssem.at[17], rsem.at[17], {"kv": sibling})
    sent.append((wp.at[0:512], 17))
    e256, w_down = get("e256"), get("w_down")
    wait_bytes(gr, rsem.at[8])
    gu = gs[z].astype(F32)
    for j in range(7):
        gu = gu + gr[j].astype(F32)
    gate, up = gu[:, 0:448], gu[:, 448:896]
    gelu = 0.5 * gate * (1.0 + jnp.tanh(0.7978845608028654 * (gate + 0.044715 * gate * gate * gate)))
    ags[z] = (gelu * up).astype(BF16)
    to_seq(lambda o: ags.at[z], lambda d: ags.at[z], 9, ags.at[0:7])
    cand = get("cand")
    for n in range(5):
        for k in range(2):
            ids = cand[n, 2 * core + k]
            if n == 0:
                tokb[:, 48 * k : 48 * k + 48] = ids
            else:
                at = 96 * (n - 1) + 48 * k
                tokd[:, at : at + 48] = ids
    lf[...] = jnp.zeros_like(lf)
    biasf[...] = jnp.zeros_like(biasf)
    biasf[0:4, 0:112] = get("bias")[...]
    accb[...] = jnp.zeros_like(accb)
    accd[...] = jnp.zeros_like(accd)
    wait_bytes(ags.at[0:7], rsem.at[9])
    for j in range(8):
        acts[24 * j : 24 * j + 24, :] = ags[j].astype(F32)
    act = dot(e256[...], acts[...].astype(BF16)).astype(BF16)
    out = dot(act, w_down[...])
    for j in range(32):
        ds[j] = out[8 * j : 8 * j + 8, :].astype(BF16)
    to_plane(lambda q: ds.at[q], lambda d: dsr.at[d - 1], 10, dsr)
    gain = get("g_fpost")[...]
    wait_bytes(dsr, rsem.at[10])
    out = ds[p].astype(F32)
    for j in range(31):
        out = out + dsr[j].astype(F32)
    gained = out * gain
    ms2[...] = moments((out * out, first * gained, gained * gained, first * first))
    to_seq(lambda o: ms2, lambda d: mr2.at[d - 1], 11, mr2)
    gain = get("g_fin")[...]
    w_draft = get("w_draft")
    wait_bytes(mr2, rsem.at[11])
    tot = ms2[...]
    for j in range(7):
        tot = tot + mr2[j]
    inv = rms_inverse(tot[:, 0:1])
    second = (first + gained * inv).astype(BF16).astype(F32)
    inv = rms_inverse(tot[:, 3:4] + 2.0 * inv * tot[:, 1:2] + inv * inv * tot[:, 2:3])
    normed = (second * inv * gain).astype(BF16)
    npl[p] = normed
    to_plane(lambda q: npl.at[p], lambda d: npl.at[p], 12, npl.at[0:31])
    nz[z] = dot(normed, spread[0:448, 0:512]).astype(BF16)
    to_seq(lambda o: nz.at[z], lambda d: nz.at[z], 13, nz.at[0:7])
    wait_bytes(npl.at[0:31], rsem.at[12])
    for j in range(32):
        xf[8 * j : 8 * j + 8, :] = npl[j].astype(F32)
    rows192 = dot(p192[...], xf[...].astype(BF16)).astype(BF16)
    for i in range(4):
        lf[i, :, 0:112] = dot(rows192, w_draft[i])
    for j in range(8):
        for i in range(4):
            dsl[j, i] = lf[i, 24 * j : 24 * j + 24, :].astype(BF16)
    to_seq(lambda o: dsl.at[o], lambda d: dslr.at[d - 1], 14, dslr)
    wait_bytes(nz.at[0:7], rsem.at[13])
    for j in range(8):
        nzs[:, 512 * j : 512 * j + 512] = nz[j].astype(F32)
    half = div(y, 2)
    slot = kv * 2 + rem(y, 2)
    nbo[...] = nzs[...].astype(BF16)

    @pl.loop(0, 16)
    def _(d):
        q = rem(x * 4 + y + d, 16)
        target = 2 * div(q, 4) + half
        to_me = (d == 0) & (half == core)

        @pl.when(jnp.logical_not(to_me))
        def _():
            send(nbo, nb.at[slot], ssem.at[15], rsem.at[15], {"kv": target, "vocab": rem(q, 4)})

        @pl.when(to_me)
        def _():
            pltpu.make_async_copy(nbo, nb.at[slot], rsem.at[15]).start()

    sent.append((nb.at[0:15], 15))
    wait_bytes(dslr, rsem.at[14])
    for i in range(4):
        lifted = dsl[z, i].astype(F32)
        for j in range(7):
            lifted = lifted + dslr[j, i].astype(F32)
        lifted = lifted + biasf[i : i + 1, :]
        zbo[i] = (lifted / (1.0 + jnp.exp(-lifted))).astype(BF16)
    reader = 2 * x + div(z, 4)
    landing = zb.at[core, rem(z, 4)]
    for d in range(8):
        other = rem(z + d, 8)
        if d:
            send(zbo, landing, ssem.at[16], rsem.at[16], {"kv": reader, "seq": other})
    keep = core == div(z, 4)

    @pl.when(jnp.logical_not(keep))
    def _():
        send(zbo, landing, ssem.at[16], rsem.at[16], {"kv": sibling})

    @pl.when(keep)
    def _():
        pltpu.make_async_copy(zbo, landing, rsem.at[16]).start()

    sent.append((zb.at[0, 0:4], 16))
    sent.append((zb.at[0, 0:3], 16))
    wait_bytes(zb, rsem.at[16])

    def block(s, o, t, part=None):
        bx, by = (x + o, y + t) if s == 0 else (x + t, y + o)
        at = pl.multiple_of(((2 * rem(bx + 4, 4) + s) * 4 + rem(by + 4, 4)) * 128, 128)
        if part is None:
            return big.at[:, :, pl.ds(at, 128)]
        return big.at[2 * part : 2 * part + 2, :, pl.ds(at, 128)]

    def neighbour(axis, step):
        if axis == 0:
            return {"kv": rem(kv + 2 * step + 8, 8)}
        return {"vocab": rem(y + step + 4, 4)}

    def ring(ref, s, axis, step, sem):
        send(ref, ref, sring.at[s], sem, neighbour(axis, step))

    offsets = (0, -1, 1, 2)

    def second_axis(s, oi):
        ref = block(s, offsets[oi], 0)
        ring(ref, s, 1 - s, 1, r2.at[s, oi, 0])
        ring(ref, s, 1 - s, -1, r2.at[s, oi, 1])

    def pass_on(s, oi):
        wait_bytes(block(s, 0, 0), r2.at[s, oi, 0])
        ring(block(s, offsets[oi], -1, 0), s, 1 - s, 1, r2h.at[s, oi, 0])
        wait_bytes(block(s, 0, 0), r2.at[s, oi, 1])
        ring(block(s, offsets[oi], 1, 1), s, 1 - s, -1, r2h.at[s, oi, 1])

    for s in range(2):
        for i in range(4):
            for j in range(4):
                bf[i, 24 * j : 24 * j + 24, :] = zb[s, j, i].astype(F32)
        own = block(s, 0, 0)
        for i in range(4):
            own[i] = bf[i].astype(BF16)
        ring(own, s, s, 1, r1.at[s, 0])
        ring(own, s, s, -1, r1.at[s, 1])
        second_axis(s, 0)

    mine = ((kv * 8 + z) * 4 + y) * 512
    theirs = ((sibling * 8 + z) * 4 + y) * 512

    def score(raw, ids, acc, lanes, i):
        logits = LOGIT_CAP * jnp.tanh(raw * (1.0 / LOGIT_CAP))
        entry = iota(raw.shape, 0)
        wanted = ids - (mine + 256 * i if i < 2 else theirs + 256 * (i - 2))
        for c in range(8):
            hit = entry == wanted[c : c + 1, :]
            acc[c : c + 1, 0:lanes] += jnp.sum(jnp.where(hit, logits, 0.0), axis=0, keepdims=True)
        acc[8:9, 0:lanes] += jnp.sum(jnp.exp(logits), axis=0, keepdims=True)

    def base(i):
        raw = dot_nt(wp[256 * i : 256 * i + 256, :], bbase[...])
        for d in range(4):
            base4[256 * i : 256 * i + 256, 96 * d : 96 * d + 96] = raw
        score(raw, tokb[:, 0:96], accb, 96, i)

    p96 = get("p96")
    for s in range(2):
        wait_bytes(block(s, 0, 0), r1.at[s, 0])
        ring(block(s, -1, 0, 0), s, s, 1, r1.at[s, 2])
        second_axis(s, 1)
    for s in range(2):
        wait_bytes(block(s, 0, 0), r1.at[s, 1])
        ring(block(s, 1, 0, 1), s, s, -1, r1.at[s, 3])
        second_axis(s, 2)
    for s in range(2):
        pass_on(s, 0)
    for s in range(2):
        wait_bytes(block(s, 0, 0, 0), r1.at[s, 2])
        wait_bytes(block(s, 0, 0, 1), r1.at[s, 3])
        second_axis(s, 3)
    wait_bytes(nb, rsem.at[15])
    for t in range(16):
        basef[8 * t : 8 * t + 8, :] = nb[t].astype(F32)
    bbase[...] = dot(p96[...], basef[...].astype(BF16)).astype(BF16)
    wait_bytes(wp.at[0:512], rsem.at[17])
    base(0)
    for s in range(2):
        pass_on(s, 1)
    base(1)
    for s in range(2):
        pass_on(s, 2)
    base(2)
    for s in range(2):
        pass_on(s, 3)
    base(3)
    for s in range(2):
        for oi in range(4):
            wait_bytes(block(s, 0, 0, 0), r2h.at[s, oi, 0])
            wait_bytes(block(s, 0, 0, 1), r2h.at[s, oi, 1])

    for i in range(4):
        rows = slice(256 * i, 256 * i + 256)
        raw = dot_nt(wp[rows, :], big[...].reshape(384, 4096)) + base4[rows, :]
        score(raw, tokd[...], accd, 384, i)

    rz[:, 0:128] = accb[...].astype(BF16)
    rz[:, 128:512] = accd[...].astype(BF16)
    to_seq(lambda o: rz, lambda d: rzr.at[d - 1], 18, rzr)
    wait_bytes(rzr, rsem.at[18])
    res = rz[...].astype(F32)
    for j in range(7):
        res = res + rzr[j].astype(F32)
    rp[p] = res.astype(BF16)
    to_plane(lambda q: rp.at[p], lambda d: rp.at[p], 19, rp.at[0:31])
    wait_bytes(rp.at[0:31], rsem.at[19])
    for c in range(2):
        res = jnp.zeros((16, 512), F32)
        for x4 in range(4):
            for yy in range(4):
                res = res + rp[(2 * x4 + c) * 4 + yy].astype(F32)
        res_ref[c] = res

    for ref, s in sent:
        wait_bytes(ref, ssem.at[s])

    @pl.when(half != core)
    def _():
        wait_bytes(nbo, ssem.at[15])

    @pl.when(jnp.logical_not(keep))
    def _():
        wait_bytes(zbo, ssem.at[16])

    for s in range(2):
        wait_bytes(big.at[:, :, 0:1920], sring.at[s])


def emit_kernel(
    len_ref, path_ref, kn_ref, vn_ref, res_ref, keys_ref, values_ref,
    keys_out, values_out, logn_ref, pick_ref,
):
    step = pl.program_id(0)
    rows = keys_ref.shape[0]
    length = len_ref[0]
    start = lax.axis_index("seq") * (rows * pl.num_programs(0)) + step * rows
    keys = keys_ref[...]
    values = values_ref[...]
    keys_out[...] = keys
    values_out[...] = values

    @pl.when((start + rows > length) & (start < length + 5))
    def _():
        away = start + iota((rows, 1), 0) - length
        target = jnp.full((rows, 1), -1, jnp.int32)
        for a in range(5):
            target = jnp.where(away == a, path_ref[0, a], target)
        selector = jnp.where(iota((rows, 48), 1) == target, 1.0, 0.0).astype(BF16)
        inside = jnp.broadcast_to(target, (rows, 256)) >= 0
        for fresh, old, out in ((kn_ref, keys, keys_out), (vn_ref, values, values_out)):
            out[...] = jnp.where(inside, dot(selector, fresh[...]), old.astype(F32)).astype(BF16)

    @pl.when(step == 0)
    def _():
        for c in range(2):
            logs = jnp.log(res_ref[c, 8:9, :])
            for n in range(5):
                for k in range(2):
                    lane = 48 * k if n == 0 else 128 + 96 * (n - 1) + 48 * k
                    logn_ref[n, 2 * c + k : 2 * c + k + 1, :] = logs[:, lane : lane + 48]
                    pick_ref[n, 2 * c + k] = res_ref[c, 0:8, lane : lane + 48]


def one_hot_rows(rows, columns, places):
    table = np.zeros((rows, columns), np.float32)
    table[np.arange(rows), places] = 1.0
    return table


def tables():
    r48 = np.arange(48)
    p48 = one_hot_rows(48, 64, (r48 // 6) * 8 + r48 % 6)
    r192 = np.arange(192)
    tenant, node = r192 // 48, r192 % 48
    p192 = one_hot_rows(192, 256, ((node // 6) * 4 + tenant) * 8 + node % 6)
    r96 = np.arange(96)
    tenant, node = r96 // 48, r96 % 48
    p96 = one_hot_rows(96, 128, ((node // 6) * 2 + tenant) * 8 + node % 6)
    return p48, p192, p96


def vmem(shape, dtype=BF16):
    return pltpu.VMEM(shape, dtype)


VM = pl.BlockSpec(memory_space=pltpu.VMEM)
SM = pl.BlockSpec(memory_space=pltpu.SMEM)
ANY = pl.BlockSpec(memory_space=pl.ANY)
DMA = pltpu.SemaphoreType.DMA


HBM = pl.BlockSpec(memory_space=pltpu.HBM)


def local(
    hidden_state,
    input_projection,
    output_projection,
    norm_pre_attention,
    norm_post_attention,
    norm_pre_feedforward,
    norm_post_feedforward,
    norm_final,
    cache_keys,
    cache_values,
    cache_length,
    ancestors,
    accepted_path,
    gate_up_weight,
    down_weight,
    draft_weight,
    draft_bias,
    vocab_weight,
    candidate_tokens,
):
    p48, p192, p96 = (jnp.asarray(t, BF16) for t in tables())
    frequency = jnp.asarray(
        (10000.0 ** (-2.0 * np.arange(128, dtype=np.float64) / 256)).astype(np.float32)
    )
    slots = cache_keys.shape[1]
    keys = cache_keys.reshape(slots, 256)
    values = cache_values.reshape(slots, 256)
    arrays = dict(
        h=hidden_state.reshape(6, 448),
        p48=p48,
        g_att=norm_pre_attention.reshape(1, 448),
        w_in=input_projection.reshape(448, 1024),
        freq=frequency.reshape(1, 128),
        anc=ancestors[0],
        keys=keys,
        values=values,
        e64=p48.T,
        w_out=output_projection[0].T,
        g_post=norm_post_attention.reshape(1, 448),
        g_pre=norm_pre_feedforward.reshape(1, 448),
        p192=p192,
        w_gu=gate_up_weight.reshape(448, 896),
        e256=p192.T,
        w_down=down_weight,
        g_fpost=norm_post_feedforward.reshape(1, 448),
        g_fin=norm_final.reshape(1, 448),
        w_draft=draft_weight,
        bias=draft_bias,
        cand=jnp.transpose(candidate_tokens, (0, 2, 3, 1)),
        p96=p96,
        w_voc=vocab_weight,
    )
    operands = [arrays[name] for name in LOADS]
    new_keys, new_values, result = pl.pallas_call(
        step_kernel,
        name="step",
        out_shape=(
            jax.ShapeDtypeStruct((48, 256), BF16),
            jax.ShapeDtypeStruct((48, 256), BF16),
            jax.ShapeDtypeStruct((2, 16, 512), F32),
        ),
        in_specs=[SM] + [HBM] * len(LOADS),
        out_specs=(VM, VM, VM),
        scratch_shapes=[vmem(a.shape, a.dtype) for a in operands] + [
            vmem((1024, 4096)), vmem((896, 1024)), vmem((8, 448), F32), vmem((8, 8, 448)),
            vmem((64, 448), F32), vmem((8, 64, 128)), vmem((7, 64, 128)), vmem((8, 48, 128)),
            vmem((96, 256)),
            vmem((96, 1), F32), vmem((96, 256), F32), vmem((8, 40, 128)), vmem((7, 40, 128)),
            vmem((8, 24, 128)), vmem((48, 512), F32), vmem((8, 8, 448)), vmem((7, 8, 448)),
            vmem((8, 128), F32), vmem((7, 8, 128), F32), vmem((32, 8, 448)), vmem((256, 448), F32),
            vmem((8, 24, 896)), vmem((7, 24, 896)), vmem((8, 24, 448)), vmem((192, 448), F32),
            vmem((32, 8, 448)), vmem((31, 8, 448)),
            vmem((8, 128), F32), vmem((7, 8, 128), F32), vmem((32, 8, 448)), vmem((8, 8, 512)),
            vmem((8, 4096), F32), vmem((8, 4096)), vmem((16, 8, 4096)),
            vmem((4, 192, 128), F32), vmem((8, 4, 24, 128)), vmem((7, 4, 24, 128)),
            vmem((8, 128), F32), vmem((4, 24, 128)), vmem((2, 4, 4, 24, 128)),
            vmem((4, 96, 128), F32), vmem((4, 96, 4096)), vmem((128, 4096), F32), vmem((96, 4096)),
            vmem((1024, 384), F32), vmem((8, 128), jnp.int32), vmem((8, 384), jnp.int32),
            vmem((16, 512)), vmem((7, 16, 512)), vmem((32, 16, 512)),
            vmem((16, 128), F32), vmem((16, 384), F32),
            DMA((len(LOADS),)), DMA((20,)), DMA((20,)), DMA((2,)), DMA((2, 4)), DMA((2, 4, 2)),
            DMA((2, 4, 2)),
        ],
        compiler_params=pltpu.CompilerParams(
            collective_id=0, has_side_effects=True, vmem_limit_bytes=62 << 20
        ),
    )(cache_length, *operands)
    block = 512
    rowspec = pl.BlockSpec((block, 256), lambda i: (i, 0))

    def whole(shape):
        return pl.BlockSpec(shape, lambda i: (0,) * len(shape))

    keys_updated, values_updated, log_normalizer, picked = pl.pallas_call(
        emit_kernel,
        name="emit",
        grid=(slots // block,),
        out_shape=(
            jax.ShapeDtypeStruct((slots, 256), BF16),
            jax.ShapeDtypeStruct((slots, 256), BF16),
            jax.ShapeDtypeStruct((5, 4, 48), F32),
            jax.ShapeDtypeStruct((5, 4, 8, 48), F32),
        ),
        in_specs=[
            SM, SM, whole((48, 256)), whole((48, 256)), whole((2, 16, 512)), rowspec, rowspec,
        ],
        out_specs=(rowspec, rowspec, whole((5, 4, 48)), whole((5, 4, 8, 48))),
        compiler_params=pltpu.CompilerParams(vmem_limit_bytes=62 << 20),
    )(cache_length, accepted_path, new_keys, new_values, result, keys, values)
    return (
        keys_updated.reshape(cache_keys.shape),
        values_updated.reshape(cache_values.shape),
        jnp.transpose(log_normalizer, (0, 2, 1)),
        jnp.transpose(picked, (0, 3, 1, 2)),
    )


def solution(mesh):
    placed = (
        P("kv", "vocab", "seq"),
        P("seq", "kv", None),
        P("kv", None, "seq"),
        P("seq"),
        P("seq"),
        P("seq"),
        P("seq"),
        P("seq"),
        P("vocab", "seq", "kv", None),
        P("vocab", "seq", "kv", None),
        P("vocab"),
        P("vocab", None, None),
        P("vocab", None),
        P("seq", None, ("kv", "vocab")),
        P(("kv", "vocab"), "seq"),
        P(None, "seq", ("kv", "vocab")),
        P(None, ("kv", "vocab")),
        P(("kv", "seq", "vocab"), None),
        P(),
    )
    return jax.shard_map(
        local,
        mesh=mesh,
        in_specs=placed,
        out_specs=(P("vocab", "seq", "kv", None), P("vocab", "seq", "kv", None), P(), P()),
        check_vma=False,
    )
```

time: 777 us -> 157 us (0.20)
  blocking collectives: 346 us -> 0 us
  waiting for transfers between devices: 329 us -> 0 us
  Pallas kernels: 0 us -> 152 us
  starting transfers between devices: 31.2 us -> 0 us
  matrix products: 26.7 us -> 0 us
  between operations: 16.9 us -> 1.44 us
  local copies, waits for them, and re-layouts: 16 us -> 3.38 us
  other arithmetic: 9.93 us -> 0 us
    psum x4 -> x0, waiting for transfers between devices: 246 us -> none  [the longest x1 73.8 us: local(): lax.psum((numerator, jnp.sum(weights, axis=-1)), 'seq')]
    pallas_call x0 -> x2, Pallas kernels: none -> 152 us  [the longest x1 148 us: local(): pl.pallas_call(step_kernel, name='step', out_shape=(jax.ShapeDtypeStruct(...]
    psum x7 -> x0, blocking collectives: 151 us -> none  [the longest x1 76.6 us: local(): totals, picked = lax.psum((totals, picked), ('kv', 'seq', 'vocab'))]
    all_gather x3 -> x0, blocking collectives: 110 us -> none  [the longest x1 48.2 us: local(): gathered = lax.all_gather(normed, ('kv', 'vocab'), axis=0, tiled=True)]
    unnamed x2 -> x0, blocking collectives: 86.2 us -> none
    all_gather x2 -> x0, waiting for transfers between devices: 82.9 us -> none  [the longest x1 52.4 us: local(): lax.all_gather(branch, ('kv', 'vocab'), axis=2, tiled=True)]
    unnamed x10 -> x0, starting transfers between devices: 30.7 us -> none
    dot_general x13 -> x0, matrix products: 26.7 us -> none  [the longest x1 8.23 us: local(): jnp.einsum('tnc,vc->tnv', lax.all_gather(branch, ('kv', 'vocab'), axis=2,...]
  transfers between devices with their start and end apart: 16 -> 0, of which waited for: 6 -> 0; matrix products, arithmetic and copies ran while one was open for 3% -> 0% of each run, Pallas kernels for 0% -> 0%
where the time goes in v2:
time: 157 us; the launch traced here: 156 us
  Pallas kernels  152 us (97%)
  local copies, waits for them, and re-layouts  3.38 us (2%)
    pallas_call x1, Pallas kernels, local(): pl.pallas_call(step_kernel, name='step', out_shape=(jax.ShapeDtypeStruct(...  148 us
    pallas_call x1, Pallas kernels, local(): pl.pallas_call(emit_kernel, name='emit', grid=(slots // block,), out_shap...  3.99 us
    reshape x1, local copies, waits for them, and re-layouts, local(): gate_up_weight.reshape(448, 896)  3.38 us

profile of v2, /device:TPU:1, one launch (start us, length us, event | category | flops | bytes accessed | tf_op | source)
XLA Modules:
  0.0 156.4 jit_solution(6958173125261697707)
XLA Ops:
  1.3 3.4 %reshape.55.refs_13_ = bf16[448,896]{1,0:T(8,128)(2,1)} reshape(bf16[448,2,448]{2,1,0:T(2,128)(2,1)} %param.36) | data formatting | bytes 1605632 | tf_op jit(solution)/shard_map/reshape | solution.py:622
  4.7 147.6 %step.1 = (bf16[48,256]{1,0:T(8,128)(2,1)}, bf16[48,256]{1,0:T(8,128)(2,1)}, f32[2,16,512]{2,1,0:T(8,128)}) custom-call(s32[1]{0:T(128)S(6)} %copy.27.len_ref, bf16[6,448]{1,0:T(8,128)(2,1)} %bitcast.26, bf16[48,64]{1,0:T(8,128)(2,1)} %constant.8.clone.refs_1_, f32[1,448]{1,0:T(1,128)} %bitcast.27, bf16[448,1024]{1,0:T(8,128)(2,1)} %bitcast.22, ...), custom_call_target="tpu_custom_call" | custom-call | tf_op jit(solution)/shard_map/step/pallas_call | solution.py:634
  152.2 4.0 %emit.1 = (bf16[2048,256]{1,0:T(8,128)(2,1)}, bf16[2048,256]{1,0:T(8,128)(2,1)}, f32[5,4,48]{2,1,0:T(4,128)}, f32[5,4,8,48]{3,2,1,0:T(8,128)}) custom-call(s32[1]{0:T(128)S(6)} %copy.27.len_ref, s32[1,5]{1,0:T(1,128)} %path_ref.1, bf16[48,256]{1,0:T(8,128)(2,1)} %get-tuple-element.11.kn_ref, bf16[48,256]{1,0:T(8,128)(2,1)} %get-tuple-element.12.vn_ref, ...), custom_call_target="tpu_custom_call" | custom-call | tf_op jit(solution)/shard_map/emit/pallas_call | solution.py:674

commit v3 on v2

--- a/solution.py
+++ b/solution.py
@@ -79,7 +79,7 @@
 LOADS = (
     "h", "p48", "g_att", "w_in", "freq", "anc", "keys", "values", "e64", "w_out", "g_post",
     "g_pre", "p192", "w_gu", "e256", "w_down", "g_fpost", "g_fin", "w_draft", "bias", "cand",
-    "p96", "w_voc",
+    "w_voc",
 )
 
 
@@ -91,15 +91,25 @@
     (
         wp, spread, pad8, xg, xf6, ps, prc, agc, qs,
         den, num, ns, nr, ga, af, os_, orr, ms, mr, fp, xf, gs, gr, ags, acts, ds, dsr,
-        ms2, mr2, npl, nz, nzs, nbo, nb, lf, dsl, dslr, biasf, zbo, zb, bf, big, basef, bbase,
-        base4, tokb, tokd, rz, rzr, rp, accb, accd,
-        wsem, ssem, rsem, sring, r1, r2, r2h,
+        ms2, mr2, npl, nsc, nbz, lf, dsl, dslr, biasf, zbo, zb, bf, big, bbase,
+        base4, tokb, tokd, rz, rx, ry, accb, accd,
+        wgu, fin, wsem, ssem, rsem, zr, sring, r1, r2, r2h,
     ) = refs[2 * count + 3 :]
     kv, z, y = position_in_mesh()
     core = rem(kv, 2)
     x = div(kv, 2)
     p = kv * 4 + y
     sibling = kv + 1 - 2 * core
+    barrier = pltpu.get_barrier_semaphore()
+
+    @pl.loop(1, 32)
+    def _(d):
+        pl.semaphore_signal(barrier, inc=1, device_id=plane_peer(p, d)[1], device_id_type=MESH)
+
+    for d in (4, 3, 5, 2, 6, 1, 7):
+        other = rem(z + d, 8)
+        pl.semaphore_signal(barrier, inc=1, device_id={"seq": other}, device_id_type=MESH)
+        pl.semaphore_signal(barrier, inc=1, device_id={"kv": sibling, "seq": other}, device_id_type=MESH)
     copies = {}
     for i, name in enumerate(LOADS):
         copies[name] = pltpu.make_async_copy(source[name], here[name], wsem.at[i])
@@ -109,33 +119,24 @@
         copies[name].wait()
         return here[name]
 
-    barrier = pltpu.get_barrier_semaphore()
-    for d in range(1, 8):
-        other = rem(z + d, 8)
-        pl.semaphore_signal(barrier, inc=1, device_id={"seq": other}, device_id_type=MESH)
-        pl.semaphore_signal(barrier, inc=1, device_id={"kv": sibling, "seq": other}, device_id_type=MESH)
-
-    @pl.loop(1, 32)
-    def _(d):
-        pl.semaphore_signal(barrier, inc=1, device_id=plane_peer(p, d)[1], device_id_type=MESH)
-
     sent = []
 
     def to_seq(src, dst, s, total):
-        for d in range(1, 8):
+        for d in (4, 3, 5, 2, 6, 1, 7):
             other = rem(z + d, 8)
             send(src(other), dst(d), ssem.at[s], rsem.at[s], {"seq": other})
         sent.append((total, s))
 
     def to_kv(src, dst, s, total):
-        for d in range(1, 8):
+        for d in (4, 5, 3, 2, 6, 1, 7):
             other = rem(kv + d, 8)
             send(src(other), dst(d), ssem.at[s], rsem.at[s], {"kv": other})
         sent.append((total, s))
 
     def to_plane(src, dst, s, total):
-        @pl.loop(1, 32)
-        def _(d):
+        @pl.loop(0, 31)
+        def _(i):
+            d = rem(i + 14, 31) + 1
             q, peer = plane_peer(p, d)
             send(src(q), dst(d), ssem.at[s], rsem.at[s], peer)
 
@@ -160,11 +161,11 @@
     tokens = dot(p48[...], xf6[...].astype(BF16))
     squares = jnp.sum(tokens * tokens, axis=1, keepdims=True)
     row = jnp.sum(jnp.where(eye[0:48], squares, 0.0), axis=0, keepdims=True)
-    row = jnp.broadcast_to(row, (16, 128)).astype(BF16)
+    row = jnp.broadcast_to(row, (8, 128)).astype(BF16)
     part = dot((tokens * gain).astype(BF16), w_in[...])
     for j in range(8):
         ps[j, 0:48, :] = part[:, 128 * j : 128 * j + 128].astype(BF16)
-        ps[j, 48:64, :] = row
+        ps[j, 48:56, :] = row
     to_seq(lambda o: ps.at[o], lambda d: prc.at[d - 1], 1, prc)
     lane = iota((896, 1024), 1)
     inside = lane & 127
@@ -211,6 +212,15 @@
         ns[j, 0:16, :] = row
         ns[j, 16:40, :] = num[r0 : r0 + 24, c0 : c0 + 128].astype(BF16)
     to_seq(lambda o: ns.at[o], lambda d: nr.at[d - 1], 3, nr)
+    raw_gu = get("w_gu")
+
+    def relay_out(i):
+        rows = slice(112 * i, 112 * i + 112)
+        wgu[rows, 0:448] = raw_gu[rows, 0, :]
+        wgu[rows, 448:896] = raw_gu[rows, 1, :]
+
+    relay_out(0)
+    relay_out(1)
     e64, w_out = get("e64"), get("w_out")
     wait_bytes(nr, rsem.at[3])
     total = ns[z].astype(F32)
@@ -220,6 +230,8 @@
     below = jnp.sum(jnp.where(chosen, total[0:1, :], 0.0), axis=1, keepdims=True)
     ga[z] = (total[16:40, :] / below).astype(BF16)
     to_seq(lambda o: ga.at[z], lambda d: ga.at[z], 4, ga.at[0:7])
+    relay_out(2)
+    relay_out(3)
     w_voc = get("w_voc")
 
     def widen(j):
@@ -256,12 +268,12 @@
     fp[p] = (first * inv * gain).astype(BF16)
     to_plane(lambda q: fp.at[p], lambda d: fp.at[p], 7, fp.at[0:31])
     widen(0)
-    p192, w_gu = get("p192"), get("w_gu")
+    p192 = get("p192")
     wait_bytes(fp.at[0:31], rsem.at[7])
     for j in range(32):
         xf[8 * j : 8 * j + 8, :] = fp[j].astype(F32)
     rows192 = dot(p192[...], xf[...].astype(BF16)).astype(BF16)
-    gu = dot(rows192, w_gu[...])
+    gu = dot(rows192, wgu[...])
     for j in range(8):
         gs[j] = gu[24 * j : 24 * j + 24, :].astype(BF16)
     to_seq(lambda o: gs.at[o], lambda d: gr.at[d - 1], 8, gr)
@@ -292,6 +304,7 @@
     biasf[...] = jnp.zeros_like(biasf)
     biasf[0:4, 0:112] = get("bias")[...]
     accb[...] = jnp.zeros_like(accb)
+    base4[...] = jnp.zeros_like(base4)
     accd[...] = jnp.zeros_like(accd)
     wait_bytes(ags.at[0:7], rsem.at[9])
     for j in range(8):
@@ -321,73 +334,68 @@
     normed = (second * inv * gain).astype(BF16)
     npl[p] = normed
     to_plane(lambda q: npl.at[p], lambda d: npl.at[p], 12, npl.at[0:31])
-    nz[z] = dot(normed, spread[0:448, 0:512]).astype(BF16)
-    to_seq(lambda o: nz.at[z], lambda d: nz.at[z], 13, nz.at[0:7])
     wait_bytes(npl.at[0:31], rsem.at[12])
     for j in range(32):
         xf[8 * j : 8 * j + 8, :] = npl[j].astype(F32)
     rows192 = dot(p192[...], xf[...].astype(BF16)).astype(BF16)
-    for i in range(4):
-        lf[i, :, 0:112] = dot(rows192, w_draft[i])
-    for j in range(8):
-        for i in range(4):
-            dsl[j, i] = lf[i, 24 * j : 24 * j + 24, :].astype(BF16)
-    to_seq(lambda o: dsl.at[o], lambda d: dslr.at[d - 1], 14, dslr)
-    wait_bytes(nz.at[0:7], rsem.at[13])
-    for j in range(8):
-        nzs[:, 512 * j : 512 * j + 512] = nz[j].astype(F32)
-    half = div(y, 2)
-    slot = kv * 2 + rem(y, 2)
-    nbo[...] = nzs[...].astype(BF16)
-
-    @pl.loop(0, 16)
-    def _(d):
-        q = rem(x * 4 + y + d, 16)
-        target = 2 * div(q, 4) + half
-        to_me = (d == 0) & (half == core)
-
-        @pl.when(jnp.logical_not(to_me))
+    halves = (slice(0, 2), slice(2, 4))
+    for h, (lifted_sem, pair) in enumerate(((13, halves[0]), (14, halves[1]))):
+        for i in (2 * h, 2 * h + 1):
+            lf[i, :, 0:112] = dot(rows192, w_draft[i])
+            for j in range(8):
+                dsl[j, i] = lf[i, 24 * j : 24 * j + 24, :].astype(BF16)
+        to_seq(
+            lambda o: dsl.at[o, pair], lambda d: dslr.at[d - 1, pair], lifted_sem, dslr.at[:, pair]
+        )
+    nsc[0] = rows192[0:96]
+    nsc[1] = rows192[96:192]
+    reader = 2 * x + div(z, 4)
+    keep = core == div(z, 4)
+    for h, (lifted_sem, group_sem, pair) in enumerate(((13, 16, halves[0]), (14, 20, halves[1]))):
+        wait_bytes(dslr.at[:, pair], rsem.at[lifted_sem])
+        for i in (2 * h, 2 * h + 1):
+            lifted = dsl[z, i].astype(F32)
+            for j in range(7):
+                lifted = lifted + dslr[j, i].astype(F32)
+            lifted = lifted + biasf[i : i + 1, :]
+            zbo[i] = (lifted / (1.0 + jnp.exp(-lifted))).astype(BF16)
+        mine, landing = zbo.at[pair], zb.at[core, rem(z, 4), pair]
+        for d in (4, 3, 5, 2, 6, 1, 7):
+            send(mine, landing, ssem.at[group_sem], rsem.at[group_sem], {"kv": reader, "seq": rem(z + d, 8)})
+
+        @pl.when(jnp.logical_not(keep))
         def _():
-            send(nbo, nb.at[slot], ssem.at[15], rsem.at[15], {"kv": target, "vocab": rem(q, 4)})
-
-        @pl.when(to_me)
+            send(mine, landing, ssem.at[group_sem], rsem.at[group_sem], {"kv": sibling})
+
+        @pl.when(keep)
         def _():
-            pltpu.make_async_copy(nbo, nb.at[slot], rsem.at[15]).start()
-
-    sent.append((nb.at[0:15], 15))
-    wait_bytes(dslr, rsem.at[14])
-    for i in range(4):
-        lifted = dsl[z, i].astype(F32)
-        for j in range(7):
-            lifted = lifted + dslr[j, i].astype(F32)
-        lifted = lifted + biasf[i : i + 1, :]
-        zbo[i] = (lifted / (1.0 + jnp.exp(-lifted))).astype(BF16)
-    reader = 2 * x + div(z, 4)
-    landing = zb.at[core, rem(z, 4)]
-    for d in range(8):
-        other = rem(z + d, 8)
-        if d:
-            send(zbo, landing, ssem.at[16], rsem.at[16], {"kv": reader, "seq": other})
-    keep = core == div(z, 4)
-
-    @pl.when(jnp.logical_not(keep))
-    def _():
-        send(zbo, landing, ssem.at[16], rsem.at[16], {"kv": sibling})
-
-    @pl.when(keep)
-    def _():
-        pltpu.make_async_copy(zbo, landing, rsem.at[16]).start()
-
-    sent.append((zb.at[0, 0:4], 16))
-    sent.append((zb.at[0, 0:3], 16))
-    wait_bytes(zb, rsem.at[16])
-
-    def block(s, o, t, part=None):
+            pltpu.make_async_copy(mine, landing, rsem.at[group_sem]).start()
+
+        sent.append((zb.at[0, 0:4, pair], group_sem))
+        sent.append((zb.at[0, 0:3, pair], group_sem))
+    nbz[z] = nsc[core]
+
+    def along_seq(ref, step, sem):
+        send(ref, ref, ssem.at[15], sem, {"seq": rem(z + step + 8, 8)})
+
+    sent.append((nbz.at[0:7], 15))
+    along_seq(nbz.at[z], 1, zr.at[0, 0])
+    along_seq(nbz.at[z], -1, zr.at[0, 1])
+
+    def base_on(k):
+        wait_bytes(nbz.at[0], zr.at[k - 1, 0])
+        left = nbz.at[rem(z - k + 8, 8)]
+        along_seq(left if k < 3 else left.at[0:48], 1, zr.at[k, 0])
+        wait_bytes(nbz.at[0], zr.at[k - 1, 1])
+        right = nbz.at[rem(z + k, 8)]
+        along_seq(right if k < 3 else right.at[48:96], -1, zr.at[k, 1])
+
+    def block(h, s, o, t, part=None):
         bx, by = (x + o, y + t) if s == 0 else (x + t, y + o)
         at = pl.multiple_of(((2 * rem(bx + 4, 4) + s) * 4 + rem(by + 4, 4)) * 128, 128)
         if part is None:
-            return big.at[:, :, pl.ds(at, 128)]
-        return big.at[2 * part : 2 * part + 2, :, pl.ds(at, 128)]
+            return big.at[2 * h : 2 * h + 2, :, pl.ds(at, 128)]
+        return big.at[2 * h + part : 2 * h + part + 1, :, pl.ds(at, 128)]
 
     def neighbour(axis, step):
         if axis == 0:
@@ -399,27 +407,29 @@
 
     offsets = (0, -1, 1, 2)
 
-    def second_axis(s, oi):
-        ref = block(s, offsets[oi], 0)
-        ring(ref, s, 1 - s, 1, r2.at[s, oi, 0])
-        ring(ref, s, 1 - s, -1, r2.at[s, oi, 1])
-
-    def pass_on(s, oi):
-        wait_bytes(block(s, 0, 0), r2.at[s, oi, 0])
-        ring(block(s, offsets[oi], -1, 0), s, 1 - s, 1, r2h.at[s, oi, 0])
-        wait_bytes(block(s, 0, 0), r2.at[s, oi, 1])
-        ring(block(s, offsets[oi], 1, 1), s, 1 - s, -1, r2h.at[s, oi, 1])
-
-    for s in range(2):
-        for i in range(4):
-            for j in range(4):
-                bf[i, 24 * j : 24 * j + 24, :] = zb[s, j, i].astype(F32)
-        own = block(s, 0, 0)
-        for i in range(4):
-            own[i] = bf[i].astype(BF16)
-        ring(own, s, s, 1, r1.at[s, 0])
-        ring(own, s, s, -1, r1.at[s, 1])
-        second_axis(s, 0)
+    def second_axis(h, s, oi):
+        ref = block(h, s, offsets[oi], 0)
+        ring(ref, s, 1 - s, 1, r2.at[h, s, oi, 0])
+        ring(ref, s, 1 - s, -1, r2.at[h, s, oi, 1])
+
+    def pass_on(h, s, oi):
+        wait_bytes(block(h, s, 0, 0), r2.at[h, s, oi, 0])
+        ring(block(h, s, offsets[oi], -1, 0), s, 1 - s, 1, r2h.at[h, s, oi, 0])
+        wait_bytes(block(h, s, 0, 0), r2.at[h, s, oi, 1])
+        ring(block(h, s, offsets[oi], 1, 1), s, 1 - s, -1, r2h.at[h, s, oi, 1])
+
+    both = tuple((h, s) for h in range(2) for s in range(2))
+    for h, (group_sem, pair) in enumerate(((16, halves[0]), (20, halves[1]))):
+        wait_bytes(zb.at[:, :, pair], rsem.at[group_sem])
+        for s in range(2):
+            own = block(h, s, 0, 0)
+            for i in range(2):
+                for j in range(4):
+                    bf[i, 24 * j : 24 * j + 24, :] = zb[s, j, 2 * h + i].astype(F32)
+                own[i] = bf[i].astype(BF16)
+            ring(own, s, s, 1, r1.at[h, s, 0])
+            ring(own, s, s, -1, r1.at[h, s, 1])
+            second_axis(h, s, 0)
 
     mine = ((kv * 8 + z) * 4 + y) * 512
     theirs = ((sibling * 8 + z) * 4 + y) * 512
@@ -436,76 +446,107 @@
     def base(i):
         raw = dot_nt(wp[256 * i : 256 * i + 256, :], bbase[...])
         for d in range(4):
-            base4[256 * i : 256 * i + 256, 96 * d : 96 * d + 96] = raw
+            base4[256 * i : 256 * i + 256, 96 * d : 96 * d + 96] += raw
         score(raw, tokb[:, 0:96], accb, 96, i)
 
-    p96 = get("p96")
-    for s in range(2):
-        wait_bytes(block(s, 0, 0), r1.at[s, 0])
-        ring(block(s, -1, 0, 0), s, s, 1, r1.at[s, 2])
-        second_axis(s, 1)
-    for s in range(2):
-        wait_bytes(block(s, 0, 0), r1.at[s, 1])
-        ring(block(s, 1, 0, 1), s, s, -1, r1.at[s, 3])
-        second_axis(s, 2)
-    for s in range(2):
-        pass_on(s, 0)
-    for s in range(2):
-        wait_bytes(block(s, 0, 0, 0), r1.at[s, 2])
-        wait_bytes(block(s, 0, 0, 1), r1.at[s, 3])
-        second_axis(s, 3)
-    wait_bytes(nb, rsem.at[15])
-    for t in range(16):
-        basef[8 * t : 8 * t + 8, :] = nb[t].astype(F32)
-    bbase[...] = dot(p96[...], basef[...].astype(BF16)).astype(BF16)
+    def add_columns(s, bx):
+        at = pl.ds(pl.multiple_of((2 * rem(bx + 4, 4) + s) * 512, 512), 512)
+        fresh = big[:, :, at].reshape(384, 512)
+        for i in range(4):
+            rows = slice(256 * i, 256 * i + 256)
+            base4[rows, :] += dot_nt(wp[rows, at], fresh)
+
+    def last_halves(s, oi):
+        for h in range(2):
+            wait_bytes(block(h, s, 0, 0, 0), r2h.at[h, s, oi, 0])
+            wait_bytes(block(h, s, 0, 0, 1), r2h.at[h, s, oi, 1])
+
+    for h, s in both:
+        wait_bytes(block(h, s, 0, 0), r1.at[h, s, 0])
+        ring(block(h, s, -1, 0, 0), s, s, 1, r1.at[h, s, 2])
+        second_axis(h, s, 1)
+        wait_bytes(block(h, s, 0, 0), r1.at[h, s, 1])
+        ring(block(h, s, 1, 0, 1), s, s, -1, r1.at[h, s, 3])
+        second_axis(h, s, 2)
     wait_bytes(wp.at[0:512], rsem.at[17])
-    base(0)
-    for s in range(2):
-        pass_on(s, 1)
-    base(1)
-    for s in range(2):
-        pass_on(s, 2)
-    base(2)
-    for s in range(2):
-        pass_on(s, 3)
-    base(3)
-    for s in range(2):
-        for oi in range(4):
-            wait_bytes(block(s, 0, 0, 0), r2h.at[s, oi, 0])
-            wait_bytes(block(s, 0, 0, 1), r2h.at[s, oi, 1])
-
+    base_on(1)
+    for h, s in both:
+        pass_on(h, s, 0)
+    for h, s in both:
+        wait_bytes(block(h, s, 0, 0, 0), r1.at[h, s, 2])
+        wait_bytes(block(h, s, 0, 0, 1), r1.at[h, s, 3])
+        second_axis(h, s, 3)
+    base_on(2)
+    for h, s in both:
+        pass_on(h, s, 1)
+    add_columns(1, x)
+    base_on(3)
+    for h, s in both:
+        pass_on(h, s, 2)
+    last_halves(0, 0)
+    add_columns(0, x)
+    for h, s in both:
+        pass_on(h, s, 3)
+    wait_bytes(nbz.at[0, 0:48], zr.at[3, 0])
+    wait_bytes(nbz.at[0, 0:48], zr.at[3, 1])
+    for j in range(8):
+        bbase[:, 512 * j : 512 * j + 512] = dot(nbz[j], spread[0:448, 0:512]).astype(BF16)
     for i in range(4):
-        rows = slice(256 * i, 256 * i + 256)
-        raw = dot_nt(wp[rows, :], big[...].reshape(384, 4096)) + base4[rows, :]
-        score(raw, tokd[...], accd, 384, i)
-
-    rz[:, 0:128] = accb[...].astype(BF16)
-    rz[:, 128:512] = accd[...].astype(BF16)
-    to_seq(lambda o: rz, lambda d: rzr.at[d - 1], 18, rzr)
-    wait_bytes(rzr, rsem.at[18])
-    res = rz[...].astype(F32)
-    for j in range(7):
-        res = res + rzr[j].astype(F32)
-    rp[p] = res.astype(BF16)
-    to_plane(lambda q: rp.at[p], lambda d: rp.at[p], 19, rp.at[0:31])
-    wait_bytes(rp.at[0:31], rsem.at[19])
+        base(i)
+    last_halves(0, 1)
+    add_columns(0, x - 1)
+    add_columns(1, x - 1)
+    add_columns(1, x + 1)
+    last_halves(0, 2)
+    add_columns(0, x + 1)
+    last_halves(0, 3)
+    add_columns(0, x + 2)
+    for oi in range(4):
+        last_halves(1, oi)
+    add_columns(1, x + 2)
+    for i in range(4):
+        score(base4[256 * i : 256 * i + 256, :], tokd[...], accd, 384, i)
+
+    fin[...] = jnp.zeros_like(fin)
+    fin[:, 0:96] = accb[0:8, 0:96]
+    fin[:, 128:512] = accd[0:8, :]
+    fin[0:1, 512:608] = accb[8:9, 0:96]
+    for d in range(4):
+        fin[d + 1 : d + 2, 512:608] = accd[8:9, 96 * d : 96 * d + 96]
+    rz[z] = fin[...].astype(BF16)
+    to_seq(lambda o: rz.at[z], lambda d: rz.at[z], 18, rz.at[0:7])
+    wait_bytes(rz.at[0:7], rsem.at[18])
+
+    def add_up(slots, count):
+        res = slots[0].astype(F32)
+        for j in range(1, count):
+            res = res + slots[j].astype(F32)
+        return res
+
+    rx[x] = add_up(rz, 8).astype(BF16)
+    for d in (2, 1, 3):
+        send(rx.at[x], rx.at[x], ssem.at[19], rsem.at[19], {"kv": rem(kv + 2 * d, 8)})
+    wait_bytes(rx.at[0:3], rsem.at[19])
+    ry[core * 4 + y] = add_up(rx, 4).astype(BF16)
+    place = ry.at[core * 4 + y]
+    for d in (2, 1, 3, 0):
+        other = rem(y + d, 4)
+        send(place, place, ssem.at[21], rsem.at[21], {"kv": sibling, "vocab": other})
+        if d:
+            send(place, place, ssem.at[21], rsem.at[21], {"vocab": other})
+    sent.append((rx.at[0:3], 19))
+    sent.append((ry.at[0:7], 21))
+    wait_bytes(ry.at[0:7], rsem.at[21])
     for c in range(2):
-        res = jnp.zeros((16, 512), F32)
-        for x4 in range(4):
-            for yy in range(4):
-                res = res + rp[(2 * x4 + c) * 4 + yy].astype(F32)
-        res_ref[c] = res
+        res_ref[c] = add_up(ry.at[4 * c : 4 * c + 4], 4)
 
     for ref, s in sent:
         wait_bytes(ref, ssem.at[s])
 
-    @pl.when(half != core)
-    def _():
-        wait_bytes(nbo, ssem.at[15])
-
     @pl.when(jnp.logical_not(keep))
     def _():
-        wait_bytes(zbo, ssem.at[16])
+        wait_bytes(zbo.at[halves[0]], ssem.at[16])
+        wait_bytes(zbo.at[halves[1]], ssem.at[20])
 
     for s in range(2):
         wait_bytes(big.at[:, :, 0:1920], sring.at[s])
@@ -538,11 +579,11 @@
     @pl.when(step == 0)
     def _():
         for c in range(2):
-            logs = jnp.log(res_ref[c, 8:9, :])
             for n in range(5):
+                logs = jnp.log(res_ref[c, n : n + 1, 512:608])
                 for k in range(2):
                     lane = 48 * k if n == 0 else 128 + 96 * (n - 1) + 48 * k
-                    logn_ref[n, 2 * c + k : 2 * c + k + 1, :] = logs[:, lane : lane + 48]
+                    logn_ref[n, 2 * c + k : 2 * c + k + 1, :] = logs[:, 48 * k : 48 * k + 48]
                     pick_ref[n, 2 * c + k] = res_ref[c, 0:8, lane : lane + 48]
 
 
@@ -558,10 +599,7 @@
     r192 = np.arange(192)
     tenant, node = r192 // 48, r192 % 48
     p192 = one_hot_rows(192, 256, ((node // 6) * 4 + tenant) * 8 + node % 6)
-    r96 = np.arange(96)
-    tenant, node = r96 // 48, r96 % 48
-    p96 = one_hot_rows(96, 128, ((node // 6) * 2 + tenant) * 8 + node % 6)
-    return p48, p192, p96
+    return p48, p192
 
 
 def vmem(shape, dtype=BF16):
@@ -598,7 +636,7 @@
     vocab_weight,
     candidate_tokens,
 ):
-    p48, p192, p96 = (jnp.asarray(t, BF16) for t in tables())
+    p48, p192 = (jnp.asarray(t, BF16) for t in tables())
     frequency = jnp.asarray(
         (10000.0 ** (-2.0 * np.arange(128, dtype=np.float64) / 256)).astype(np.float32)
     )
@@ -619,7 +657,7 @@
         g_post=norm_post_attention.reshape(1, 448),
         g_pre=norm_pre_feedforward.reshape(1, 448),
         p192=p192,
-        w_gu=gate_up_weight.reshape(448, 896),
+        w_gu=gate_up_weight,
         e256=p192.T,
         w_down=down_weight,
         g_fpost=norm_post_feedforward.reshape(1, 448),
@@ -627,7 +665,6 @@
         w_draft=draft_weight,
         bias=draft_bias,
         cand=jnp.transpose(candidate_tokens, (0, 2, 3, 1)),
-        p96=p96,
         w_voc=vocab_weight,
     )
     operands = [arrays[name] for name in LOADS]
@@ -637,29 +674,30 @@
         out_shape=(
             jax.ShapeDtypeStruct((48, 256), BF16),
             jax.ShapeDtypeStruct((48, 256), BF16),
-            jax.ShapeDtypeStruct((2, 16, 512), F32),
+            jax.ShapeDtypeStruct((2, 8, 640), F32),
         ),
         in_specs=[SM] + [HBM] * len(LOADS),
         out_specs=(VM, VM, VM),
         scratch_shapes=[vmem(a.shape, a.dtype) for a in operands] + [
             vmem((1024, 4096)), vmem((896, 1024)), vmem((8, 448), F32), vmem((8, 8, 448)),
-            vmem((64, 448), F32), vmem((8, 64, 128)), vmem((7, 64, 128)), vmem((8, 48, 128)),
+            vmem((64, 448), F32), vmem((8, 56, 128)), vmem((7, 56, 128)), vmem((8, 48, 128)),
             vmem((96, 256)),
             vmem((96, 1), F32), vmem((96, 256), F32), vmem((8, 40, 128)), vmem((7, 40, 128)),
             vmem((8, 24, 128)), vmem((48, 512), F32), vmem((8, 8, 448)), vmem((7, 8, 448)),
             vmem((8, 128), F32), vmem((7, 8, 128), F32), vmem((32, 8, 448)), vmem((256, 448), F32),
             vmem((8, 24, 896)), vmem((7, 24, 896)), vmem((8, 24, 448)), vmem((192, 448), F32),
             vmem((32, 8, 448)), vmem((31, 8, 448)),
-            vmem((8, 128), F32), vmem((7, 8, 128), F32), vmem((32, 8, 448)), vmem((8, 8, 512)),
-            vmem((8, 4096), F32), vmem((8, 4096)), vmem((16, 8, 4096)),
+            vmem((8, 128), F32), vmem((7, 8, 128), F32), vmem((32, 8, 448)),
+            vmem((2, 96, 448)), vmem((8, 96, 448)),
             vmem((4, 192, 128), F32), vmem((8, 4, 24, 128)), vmem((7, 4, 24, 128)),
             vmem((8, 128), F32), vmem((4, 24, 128)), vmem((2, 4, 4, 24, 128)),
-            vmem((4, 96, 128), F32), vmem((4, 96, 4096)), vmem((128, 4096), F32), vmem((96, 4096)),
+            vmem((2, 96, 128), F32), vmem((4, 96, 4096)), vmem((96, 4096)),
             vmem((1024, 384), F32), vmem((8, 128), jnp.int32), vmem((8, 384), jnp.int32),
-            vmem((16, 512)), vmem((7, 16, 512)), vmem((32, 16, 512)),
+            vmem((8, 8, 640)), vmem((4, 8, 640)), vmem((8, 8, 640)),
             vmem((16, 128), F32), vmem((16, 384), F32),
-            DMA((len(LOADS),)), DMA((20,)), DMA((20,)), DMA((2,)), DMA((2, 4)), DMA((2, 4, 2)),
-            DMA((2, 4, 2)),
+            vmem((448, 896)), vmem((8, 640), F32),
+            DMA((len(LOADS),)), DMA((23,)), DMA((23,)), DMA((4, 2)), DMA((2,)), DMA((2, 2, 4)), DMA((2, 2, 4, 2)),
+            DMA((2, 2, 4, 2)),
         ],
         compiler_params=pltpu.CompilerParams(
             collective_id=0, has_side_effects=True, vmem_limit_bytes=62 << 20
@@ -682,7 +720,7 @@
             jax.ShapeDtypeStruct((5, 4, 8, 48), F32),
         ),
         in_specs=[
-            SM, SM, whole((48, 256)), whole((48, 256)), whole((2, 16, 512)), rowspec, rowspec,
+            SM, SM, whole((48, 256)), whole((48, 256)), whole((2, 8, 640)), rowspec, rowspec,
         ],
         out_specs=(rowspec, rowspec, whole((5, 4, 48)), whole((5, 4, 8, 48))),
         compiler_params=pltpu.CompilerParams(vmem_limit_bytes=62 << 20),

time: 157 us -> 144 us (0.917)
  Pallas kernels: 152 us -> 143 us
  local copies, waits for them, and re-layouts: 3.38 us -> 0 us
    pallas_call x1, Pallas kernels: 148 us -> 139 us  [local(): pl.pallas_call(step_kernel, name='step', out_shape=(jax.ShapeDtypeStruct(...]
    reshape x1 -> x0, local copies, waits for them, and re-layouts: 3.38 us -> none  [local(): gate_up_weight.reshape(448, 896)]
where the time goes in v3:
time: 144 us
  Pallas kernels  143 us (99%)
  between operations  1.45 us (1%)
    pallas_call x1, Pallas kernels, local(): pl.pallas_call(step_kernel, name='step', out_shape=(jax.ShapeDtypeStruct(...  139 us
    pallas_call x1, Pallas kernels, local(): pl.pallas_call(emit_kernel, name='emit', grid=(slots // block,), out_shap...  3.98 us

profile of v3, /device:TPU:1, one launch (start us, length us, event | category | flops | bytes accessed | tf_op | source)
XLA Modules:
  0.0 144.1 jit_solution(9995529551439603101)
XLA Ops:
  1.3 138.7 %step.1 = (bf16[48,256]{1,0:T(8,128)(2,1)}, bf16[48,256]{1,0:T(8,128)(2,1)}, f32[2,8,640]{2,1,0:T(8,128)}) custom-call(s32[1]{0:T(128)S(6)} %copy.26.len_ref, bf16[6,448]{1,0:T(8,128)(2,1)} %bitcast.26, bf16[48,64]{1,0:T(8,128)(2,1)} %constant.6.clone.refs_1_, f32[1,448]{1,0:T(1,128)} %bitcast.27, bf16[448,1024]{1,0:T(8,128)(2,1)} %bitcast.22, ...), custom_call_target="tpu_custom_call" | custom-call | tf_op jit(solution)/shard_map/step/pallas_call | solution.py:671
  140.0 4.0 %emit.1 = (bf16[2048,256]{1,0:T(8,128)(2,1)}, bf16[2048,256]{1,0:T(8,128)(2,1)}, f32[5,4,48]{2,1,0:T(4,128)}, f32[5,4,8,48]{3,2,1,0:T(8,128)}) custom-call(s32[1]{0:T(128)S(6)} %copy.26.len_ref, s32[1,5]{1,0:T(1,128)} %path_ref.1, bf16[48,256]{1,0:T(8,128)(2,1)} %get-tuple-element.11.kn_ref, bf16[48,256]{1,0:T(8,128)(2,1)} %get-tuple-element.12.vn_ref, ...), custom_call_target="tpu_custom_call" | custom-call | tf_op jit(solution)/shard_map/emit/pallas_call | solution.py:712

commit v4 on v3

--- a/solution.py
+++ b/solution.py
@@ -93,7 +93,7 @@
         den, num, ns, nr, ga, af, os_, orr, ms, mr, fp, xf, gs, gr, ags, acts, ds, dsr,
         ms2, mr2, npl, nsc, nbz, lf, dsl, dslr, biasf, zbo, zb, bf, big, bbase,
         base4, tokb, tokd, rz, rx, ry, accb, accd,
-        wgu, fin, wsem, ssem, rsem, zr, sring, r1, r2, r2h,
+        wgu, fin, pad6, wsem, ssem, rsem, zr, sring, r1, r2, r2h,
     ) = refs[2 * count + 3 :]
     kv, z, y = position_in_mesh()
     core = rem(kv, 2)
@@ -143,6 +143,8 @@
         sent.append((total, s))
 
     pad8[...] = jnp.zeros_like(pad8)
+    pad6[...] = jnp.zeros_like(pad6)
+    xf[...] = jnp.zeros_like(xf)
     pad8[0:6, :] = get("h")[...].astype(F32)
     xg[kv] = pad8[...].astype(BF16)
     pl.semaphore_wait(barrier, 45)
@@ -265,13 +267,13 @@
     inv = rms_inverse(tot[:, 0:1])
     first = (hidden + gained * inv).astype(BF16).astype(F32)
     inv = rms_inverse(tot[:, 3:4] + 2.0 * inv * tot[:, 1:2] + inv * inv * tot[:, 2:3])
-    fp[p] = (first * inv * gain).astype(BF16)
+    fp[p] = (first * inv * gain)[0:6].astype(BF16)
     to_plane(lambda q: fp.at[p], lambda d: fp.at[p], 7, fp.at[0:31])
     widen(0)
     p192 = get("p192")
     wait_bytes(fp.at[0:31], rsem.at[7])
     for j in range(32):
-        xf[8 * j : 8 * j + 8, :] = fp[j].astype(F32)
+        xf[8 * j : 8 * j + 6, :] = fp[j].astype(F32)
     rows192 = dot(p192[...], xf[...].astype(BF16)).astype(BF16)
     gu = dot(rows192, wgu[...])
     for j in range(8):
@@ -312,13 +314,15 @@
     act = dot(e256[...], acts[...].astype(BF16)).astype(BF16)
     out = dot(act, w_down[...])
     for j in range(32):
-        ds[j] = out[8 * j : 8 * j + 8, :].astype(BF16)
+        ds[j] = out[8 * j : 8 * j + 6, :].astype(BF16)
     to_plane(lambda q: ds.at[q], lambda d: dsr.at[d - 1], 10, dsr)
     gain = get("g_fpost")[...]
     wait_bytes(dsr, rsem.at[10])
     out = ds[p].astype(F32)
     for j in range(31):
         out = out + dsr[j].astype(F32)
+    pad6[0:6, :] = out
+    out = pad6[...]
     gained = out * gain
     ms2[...] = moments((out * out, first * gained, gained * gained, first * first))
     to_seq(lambda o: ms2, lambda d: mr2.at[d - 1], 11, mr2)
@@ -331,12 +335,12 @@
     inv = rms_inverse(tot[:, 0:1])
     second = (first + gained * inv).astype(BF16).astype(F32)
     inv = rms_inverse(tot[:, 3:4] + 2.0 * inv * tot[:, 1:2] + inv * inv * tot[:, 2:3])
-    normed = (second * inv * gain).astype(BF16)
-    npl[p] = normed
+    normed = second * inv * gain
+    npl[p] = normed[0:6].astype(BF16)
     to_plane(lambda q: npl.at[p], lambda d: npl.at[p], 12, npl.at[0:31])
     wait_bytes(npl.at[0:31], rsem.at[12])
     for j in range(32):
-        xf[8 * j : 8 * j + 8, :] = npl[j].astype(F32)
+        xf[8 * j : 8 * j + 6, :] = npl[j].astype(F32)
     rows192 = dot(p192[...], xf[...].astype(BF16)).astype(BF16)
     halves = (slice(0, 2), slice(2, 4))
     for h, (lifted_sem, pair) in enumerate(((13, halves[0]), (14, halves[1]))):
@@ -684,10 +688,10 @@
             vmem((96, 256)),
             vmem((96, 1), F32), vmem((96, 256), F32), vmem((8, 40, 128)), vmem((7, 40, 128)),
             vmem((8, 24, 128)), vmem((48, 512), F32), vmem((8, 8, 448)), vmem((7, 8, 448)),
-            vmem((8, 128), F32), vmem((7, 8, 128), F32), vmem((32, 8, 448)), vmem((256, 448), F32),
+            vmem((8, 128), F32), vmem((7, 8, 128), F32), vmem((32, 6, 448)), vmem((256, 448), F32),
             vmem((8, 24, 896)), vmem((7, 24, 896)), vmem((8, 24, 448)), vmem((192, 448), F32),
-            vmem((32, 8, 448)), vmem((31, 8, 448)),
-            vmem((8, 128), F32), vmem((7, 8, 128), F32), vmem((32, 8, 448)),
+            vmem((32, 6, 448)), vmem((31, 6, 448)),
+            vmem((8, 128), F32), vmem((7, 8, 128), F32), vmem((32, 6, 448)),
             vmem((2, 96, 448)), vmem((8, 96, 448)),
             vmem((4, 192, 128), F32), vmem((8, 4, 24, 128)), vmem((7, 4, 24, 128)),
             vmem((8, 128), F32), vmem((4, 24, 128)), vmem((2, 4, 4, 24, 128)),
@@ -695,7 +699,7 @@
             vmem((1024, 384), F32), vmem((8, 128), jnp.int32), vmem((8, 384), jnp.int32),
             vmem((8, 8, 640)), vmem((4, 8, 640)), vmem((8, 8, 640)),
             vmem((16, 128), F32), vmem((16, 384), F32),
-            vmem((448, 896)), vmem((8, 640), F32),
+            vmem((448, 896)), vmem((8, 640), F32), vmem((8, 448), F32),
             DMA((len(LOADS),)), DMA((23,)), DMA((23,)), DMA((4, 2)), DMA((2,)), DMA((2, 2, 4)), DMA((2, 2, 4, 2)),
             DMA((2, 2, 4, 2)),
         ],
@@ -703,7 +707,7 @@
             collective_id=0, has_side_effects=True, vmem_limit_bytes=62 << 20
         ),
     )(cache_length, *operands)
-    block = 512
+    block = 1024
     rowspec = pl.BlockSpec((block, 256), lambda i: (i, 0))
 
     def whole(shape):

time: 144 us -> 143 us (level)
  no operation moved by 1% of the time
where the time goes in v4:
time: 143 us
  Pallas kernels  142 us (99%)
  between operations  1.45 us (1%)
    pallas_call x1, Pallas kernels, local(): pl.pallas_call(step_kernel, name='step', out_shape=(jax.ShapeDtypeStruct(...  139 us

profile of v4, /device:TPU:1, one launch (start us, length us, event | category | flops | bytes accessed | tf_op | source)
XLA Modules:
  0.0 143.1 jit_solution(15471758808210542697)
XLA Ops:
  1.3 138.8 %step.1 = (bf16[48,256]{1,0:T(8,128)(2,1)}, bf16[48,256]{1,0:T(8,128)(2,1)}, f32[2,8,640]{2,1,0:T(8,128)}) custom-call(s32[1]{0:T(128)S(6)} %copy.26.len_ref, bf16[6,448]{1,0:T(8,128)(2,1)} %bitcast.26, bf16[48,64]{1,0:T(8,128)(2,1)} %constant.6.clone.refs_1_, f32[1,448]{1,0:T(1,128)} %bitcast.27, bf16[448,1024]{1,0:T(8,128)(2,1)} %bitcast.22, ...), custom_call_target="tpu_custom_call" | custom-call | tf_op jit(solution)/shard_map/step/pallas_call | solution.py:675
  140.1 2.9 %emit.1 = (bf16[2048,256]{1,0:T(8,128)(2,1)}, bf16[2048,256]{1,0:T(8,128)(2,1)}, f32[5,4,48]{2,1,0:T(4,128)}, f32[5,4,8,48]{3,2,1,0:T(8,128)}) custom-call(s32[1]{0:T(128)S(6)} %copy.26.len_ref, s32[1,5]{1,0:T(1,128)} %path_ref.1, bf16[48,256]{1,0:T(8,128)(2,1)} %get-tuple-element.11.kn_ref, bf16[48,256]{1,0:T(8,128)(2,1)} %get-tuple-element.12.vn_ref, ...), custom_call_target="tpu_custom_call" | custom-call | tf_op jit(solution)/shard_map/emit/pallas_call | solution.py:716
